TPU v7x, 128 devices: a whole 4x4x4 slice. The times are simulated.
128 devices in a mesh: expert: 16 (over z, x), group: 8 (over y, core).
Axes of the slice: x: 4, y: 4, z: 4, core: 2. Of those that a mesh axis runs over, the one named last changes fastest.
Arguments:
- activations: bfloat16 [16384, 2048], P(('expert', 'group')), may hold values from -24 to 24
- out_grad: bfloat16 [16384, 2048], P(('expert', 'group')), may hold values from -24 to 24
- combine_weights: bfloat16 [16384, 4], P(('expert', 'group')), may hold values from 0.099609375 to 0.5
- expert_ids: int32 [16384, 4], P(('expert', 'group')), may hold values from 0 to 15, all different within a row; in each aligned block of 128 rows (0 to 127, 128 to 255, ...) at most 96 rows name the same one
- gate_up_weight: bfloat16 [16, 2048, 1024], P('expert'), may hold values from -0.125 to 0.125
- down_weight: bfloat16 [16, 2048, 512], P('expert'), may hold values from -0.25 to 0.25
Outputs:
- grad_input: bfloat16 [16384, 2048], P(('expert', 'group'))
- grad_combine: bfloat16 [16384, 4], P(('expert', 'group'))
- grad_gate_up: float32 [16, 2048, 1024], P('expert', 'group')
- grad_down: float32 [16, 2048, 512], P('expert', 'group')
Inputs may be any that keep to these rules, and one draw needn't show every extreme that they name: `expert_ids`: each row names 4 different experts. Within the 128 rows of one device no expert is named more than 96 times, and in some device's rows an expert is named exactly 96 times.
All inputs are finite; a program needn't handle non-finite values.
Results may differ from a plain program's by a relative error of at most 0.0064.
Values may be sent and summed in bfloat16 or wider, within the bound.
A program may use at most 128 MiB of HBM per device.

v0:
```python
import jax
import jax.numpy as jnp
from jax import lax
from jax.sharding import PartitionSpec as P


def assign_slots(flat_ids, expert_count, capacity):
    columns = lax.broadcasted_iota(jnp.int32, (1, expert_count), 1)
    onehot = (flat_ids[:, None] == columns).astype(jnp.int32)
    before = jnp.cumsum(onehot, axis=0) - onehot
    rank_in = jnp.sum(before * onehot, axis=1)
    return flat_ids * capacity + rank_in


def owners_of(positions, total_slots, filler):
    table = jnp.full((total_slots + 1,), filler, jnp.int32)
    filled = table.at[positions].set(lax.iota(jnp.int32, positions.shape[0]))
    return filled[:total_slots]


def padded_rows(values, index):
    zero_row = jnp.zeros((1,) + values.shape[1:], values.dtype)
    return jnp.concatenate([values, zero_row], axis=0)[index]


def body(activations, out_grad, combine_weights, expert_ids, gate_up_weight, down_weight):
    tok_count = activations.shape[0]
    feature_dim = activations.shape[1]
    top_count = expert_ids.shape[1]
    experts_all = lax.axis_size("expert")
    capacity = min(tok_count, 3 * tok_count * top_count // experts_all)
    total_slots = experts_all * capacity
    flat_ids = expert_ids.reshape(-1)
    assign_count = flat_ids.shape[0]
    slots = assign_slots(flat_ids, experts_all, capacity)
    owners = owners_of(slots, total_slots, assign_count)
    token_row = jnp.where(owners < assign_count, owners // top_count, tok_count)
    send_x = padded_rows(activations, token_row).reshape(experts_all, capacity, feature_dim)
    send_g = padded_rows(out_grad, token_row).reshape(experts_all, capacity, feature_dim)
    send_w = padded_rows(combine_weights.reshape(-1), owners).reshape(experts_all, capacity)
    arrived = (
        lax.all_to_all(send_x, "expert", split_axis=0, concat_axis=0, tiled=True),
        lax.all_to_all(send_g, "expert", split_axis=0, concat_axis=0, tiled=True),
        lax.all_to_all(send_w, "expert", split_axis=0, concat_axis=0, tiled=True),
    )
    rows_x = arrived[0].reshape(total_slots, feature_dim)
    rows_g = arrived[1].reshape(total_slots, feature_dim)
    rows_w = arrived[2].reshape(total_slots)
    weight_gu = gate_up_weight[0]
    weight_down = down_weight[0]
    hidden_dim = weight_down.shape[1]
    pre = jnp.dot(rows_x, weight_gu, preferred_element_type=jnp.float32)
    gate = pre[:, :hidden_dim]
    upper = pre[:, hidden_dim:]
    sig = jax.nn.sigmoid(gate)
    hidden = (jax.nn.silu(gate) * upper).astype(jnp.bfloat16)
    expert_out = lax.dot_general(
        hidden, weight_down, (((1,), (1,)), ((), ())), preferred_element_type=jnp.float32
    )
    prob_grad = jnp.sum(rows_g.astype(jnp.float32) * expert_out, axis=1).astype(jnp.bfloat16)
    scaled = (rows_w.astype(jnp.float32)[:, None] * rows_g.astype(jnp.float32)).astype(jnp.bfloat16)
    hidden_grad = jnp.dot(scaled, weight_down, preferred_element_type=jnp.float32)
    gate_grad = hidden_grad * upper * sig * (1.0 + gate * (1.0 - sig))
    upper_grad = hidden_grad * gate * sig
    pre_grad = jnp.concatenate([gate_grad, upper_grad], axis=1).astype(jnp.bfloat16)
    slot_grad = lax.dot_general(
        pre_grad, weight_gu, (((1,), (1,)), ((), ())), preferred_element_type=jnp.float32
    ).astype(jnp.bfloat16)
    back = (
        lax.all_to_all(
            slot_grad.reshape(experts_all, capacity, feature_dim),
            "expert",
            split_axis=0,
            concat_axis=0,
            tiled=True,
        ),
        lax.all_to_all(
            prob_grad.reshape(experts_all, capacity),
            "expert",
            split_axis=0,
            concat_axis=0,
            tiled=True,
        ),
    )
    per_assign = (
        back[0].reshape(total_slots, feature_dim)[slots].reshape(tok_count, top_count, feature_dim)
    )
    grad_input = jnp.sum(per_assign.astype(jnp.float32), axis=1).astype(jnp.bfloat16)
    grad_combine = back[1].reshape(total_slots)[slots].reshape(tok_count, top_count)
    grad_gate_up = lax.psum_scatter(
        lax.dot_general(
            rows_x, pre_grad, (((0,), (0,)), ((), ())), preferred_element_type=jnp.float32
        ),
        "group",
        scatter_dimension=0,
        tiled=True,
    )
    grad_down = lax.psum_scatter(
        lax.dot_general(
            scaled, hidden, (((0,), (0,)), ((), ())), preferred_element_type=jnp.float32
        ),
        "group",
        scatter_dimension=0,
        tiled=True,
    )
    return (grad_input, grad_combine, grad_gate_up[None], grad_down[None])


def solution(mesh):
    placed = (
        P(("expert", "group"), None),
        P(("expert", "group"), None),
        P(("expert", "group"), None),
        P(("expert", "group"), None),
        P("expert", None, None),
        P("expert", None, None),
    )
    return jax.shard_map(
        body,
        mesh=mesh,
        in_specs=placed,
        out_specs=(
            P(("expert", "group"), None),
            P(("expert", "group"), None),
            P("expert", "group", None),
            P("expert", "group", None),
        ),
        check_vma=False,
    )
```

profile of v0, /device:TPU:1, one launch (start us, length us, event | category | flops | bytes accessed | tf_op | source)
XLA Modules:
  0.0 406.7 jit_solution(15559617457832984203)
XLA Ops:
  7.2 0.0 copy-start
  7.2 0.9 copy.25
  8.1 0.1 eq.29
  8.2 0.1 eq.25
  8.4 0.7 broadcast_multiply_fusion
  9.0 1.1 reduce-window.6
  10.2 0.2 slice_reduce_fusion
  10.5 0.1 copy.24
  10.6 0.1 mul.66
  10.7 0.1 fusion.12
  10.8 2.5 scatter_custom_fusion
  13.3 0.8 copy.23
  14.1 0.1 reshape.136
  14.2 9.5 %gather_fusion = bf16[1536]{0:T(1024)(128)(2,1)S(1)} fusion(bf16[513]{0:T(1024)(128)(2,1)S(1)} %pad_maximum_fusion.3, s32[2048]{0:T(1024)S(1)} %get-tuple-element.24), kind=kCustom, calls=%fused_computation | custom fusion | bytes 12288 | tf_op jit(solution)/shard_map/gather | solution.py:23
  23.7 0.7 all_to_all.25
  24.4 8.4 %all-to-all-start = ((bf16[16,1,96]{2,1,0:T(2,128)(2,1)}), bf16[16,1,96]{2,1,0:T(2,128)(2,1)S(1)}, u32[]{:S(2)}, u32[]{:S(2)}) async-start(bf16[16,1,96]{2,1,0:T(2,128)(2,1)} %all_to_all.25), calls=%async_computation | async-start | bytes 16384 | tf_op jit(solution)/shard_map/all_to_all | solution.py:44
  32.9 7.1 %gather_fusion.2 = bf16[1536,2048]{1,0:T(8,128)(2,1)} fusion(bf16[129,2048]{1,0:T(8,128)(2,1)S(1)} %concatenate.15, s32[2048]{0:T(1024)S(1)} %get-tuple-element.23), kind=kCustom, calls=%fused_computation.2 | custom fusion | bytes 12589056 | tf_op jit(solution)/shard_map/gather | solution.py:23
  40.0 0.0 all-to-all-done
  40.0 6.8 %all-to-all-start.2 = ((bf16[16,96,2048]{2,1,0:T(8,128)(2,1)}), bf16[16,96,2048]{2,1,0:T(8,128)(2,1)}, u32[]{:S(2)}, u32[]{:S(2)}) async-start(bf16[16,96,2048]{2,1,0:T(8,128)(2,1)} %bitcast.57), calls=%async_computation.2 | async-start | bytes 12582912 | tf_op jit(solution)/shard_map/all_to_all | solution.py:42
  46.9 7.1 %gather_fusion.1 = bf16[1536,2048]{1,0:T(8,128)(2,1)} fusion(bf16[129,2048]{1,0:T(8,128)(2,1)S(1)} %concatenate.14, s32[2048]{0:T(1024)S(1)} %get-tuple-element.23), kind=kCustom, calls=%fused_computation.1 | custom fusion | bytes 12589056 | tf_op jit(solution)/shard_map/gather | solution.py:23
  54.0 84.7 %all-to-all-done.2 = bf16[16,96,2048]{2,1,0:T(8,128)(2,1)} async-done(((bf16[16,96,2048]{2,1,0:T(8,128)(2,1)}), bf16[16,96,2048]{2,1,0:T(8,128)(2,1)}, u32[]{:S(2)}, u32[]{:S(2)}) %all-to-all-start.2) | async-done | bytes 6291488 | tf_op jit(solution)/shard_map/all_to_all | solution.py:42
  138.6 4.8 %all-to-all-start.1 = ((bf16[16,96,2048]{2,1,0:T(8,128)(2,1)}), bf16[16,96,2048]{2,1,0:T(8,128)(2,1)}, u32[]{:S(2)}, u32[]{:S(2)}) async-start(bf16[16,96,2048]{2,1,0:T(8,128)(2,1)} %bitcast.56), calls=%async_computation.1 | async-start | bytes 12582912 | tf_op jit(solution)/shard_map/all_to_all | solution.py:43
  143.4 0.2 reduce-scatter.5.cloned.1.call-start
  143.7 0.1 reshape.148
  143.8 11.8 %fusion.4 = f32[1536,1024]{0,1:T(8,128)} fusion(bf16[1536,2048]{1,0:T(8,128)(2,1)} %bitcast.8, bf16[1,2048,1024]{2,1,0:T(8,128)(2,1)} %param.10), kind=kOutput, calls=%fused_computation.14 | convolution fusion | flops 6442450944 | bytes 16777216 | tf_op jit(solution)/shard_map/dot_general | solution.py:52
  155.6 77.1 %all-to-all-done.1 = bf16[16,96,2048]{2,1,0:T(8,128)(2,1)} async-done(((bf16[16,96,2048]{2,1,0:T(8,128)(2,1)}), bf16[16,96,2048]{2,1,0:T(8,128)(2,1)}, u32[]{:S(2)}, u32[]{:S(2)}) %all-to-all-start.1) | async-done | bytes 6291488 | tf_op jit(solution)/shard_map/all_to_all | solution.py:43
  232.8 4.0 fusion
  236.8 0.6 copy-done.4
  237.4 6.5 %multiply_convert_fusion.2 = (bf16[1536,512]{0,1:T(8,128)(2,1)}, bf16[1536,512]{0,1:T(8,128)(2,1)}, bf16[1536,512]{0,1:T(8,128)(2,1)S(1)}) fusion(f32[1536,1024]{0,1:T(8,128)S(1)} %copy-done.4, bf16[1536,2048]{1,0:T(8,128)(2,1)S(1)} %bitcast.59, bf16[1,2048,512]{2,1,0:T(8,128)(2,1)S(1)} %copy-done), kind=kOutput, calls=%fused_computation.19 | convolution fusion | flops 3233808384 | bytes 19398656 | tf_op jit(solution)/shard_map/dot_general | solution.py:62
  243.8 4.4 %fusion.2 = bf16[1536,2048]{1,0:T(8,128)(2,1)S(1)} fusion(bf16[16,96,2048]{2,1,0:T(8,128)(2,1)} %all-to-all-done.1, f32[1536]{0:T(1024)S(1)} %reshape.148), kind=kLoop, calls=%fused_computation.11 | loop fusion | flops 9437184 | bytes 12589056 | tf_op jit(solution)/shard_map/convert_element_type | solution.py:61
  248.3 5.5 %fusion.21 = f32[2048,512]{1,0:T(8,128)} fusion(bf16[1536,2048]{1,0:T(8,128)(2,1)S(1)} %fusion.2, bf16[1536,512]{0,1:T(8,128)(2,1)S(1)} %get-tuple-element.18), kind=kOutput, calls=%fused_computation.56 | convolution fusion | flops 3221225472 | bytes 12058624 | tf_op jit(solution)/shard_map/dot_general | solution.py:99
  253.7 0.0 reduce-scatter.5.cloned.1.call-update
  253.8 0.3 reduce-scatter.3.cloned.1.call-start
  254.0 11.8 %fusion.9 = f32[2048,1024]{1,0:T(8,128)} fusion(bf16[1536,2048]{1,0:T(8,128)(2,1)} %bitcast.8, bf16[1536,512]{0,1:T(8,128)(2,1)} %get-tuple-element.17, bf16[1536,512]{0,1:T(8,128)(2,1)} %get-tuple-element.16), kind=kOutput, calls=%fused_computation.24 | convolution fusion | flops 6448742400 | bytes 17825792 | tf_op jit(solution)/shard_map/dot_general | solution.py:91
  265.8 0.0 reduce-scatter.3.cloned.1.call-update
  265.8 6.3 %fusion.1 = bf16[1536]{0:T(1024)(128)(2,1)S(1)} fusion(bf16[16,96,2048]{2,1,0:T(8,128)(2,1)} %all-to-all-done.1, bf16[1536,512]{0,1:T(8,128)(2,1)} %copy-done.3, bf16[1,2048,512]{2,1,0:T(8,128)(2,1)S(1)} %copy-done), kind=kOutput, calls=%fused_computation.10 | convolution fusion | flops 3230661120 | bytes 9964544 | tf_op jit(solution)/shard_map/dot_general | solution.py:57
  272.1 0.7 convert_element_type.83
  272.8 5.4 %all-to-all-start.4 = ((bf16[16,1,96]{2,1,0:T(2,128)(2,1)}), bf16[16,1,96]{2,1,0:T(2,128)(2,1)S(1)}, u32[]{:S(2)}, u32[]{:S(2)}) async-start(bf16[16,1,96]{2,1,0:T(2,128)(2,1)} %convert_element_type.83), calls=%async_computation.4 | async-start | bytes 16384 | tf_op jit(solution)/shard_map/all_to_all | solution.py:77
  278.2 11.4 %convolution_convert_fusion = bf16[1536,2048]{1,0:T(8,128)(2,1)} fusion(bf16[1,2048,1024]{2,1,0:T(8,128)(2,1)} %param.10, bf16[1536,512]{0,1:T(8,128)(2,1)} %get-tuple-element.17, bf16[1536,512]{0,1:T(8,128)(2,1)} %get-tuple-element.16), kind=kOutput, calls=%fused_computation.12 | convolution fusion | flops 6451888128 | bytes 13631488 | tf_op jit(solution)/shard_map/dot_general | solution.py:66
  289.6 6.7 %all-to-all-start.3 = ((bf16[16,96,2048]{2,1,0:T(8,128)(2,1)}), bf16[16,96,2048]{2,1,0:T(8,128)(2,1)}, u32[]{:S(2)}, u32[]{:S(2)}) async-start(bf16[16,96,2048]{2,1,0:T(8,128)(2,1)} %bitcast.58), calls=%async_computation.3 | async-start | bytes 12582912 | tf_op jit(solution)/shard_map/all_to_all | solution.py:70
  296.4 0.1 reshape.144
  296.4 3.5 gather_fusion.4
  300.0 0.1 reshape.145
  300.1 0.7 copy.30
  300.7 81.2 %all-to-all-done.3 = bf16[16,96,2048]{2,1,0:T(8,128)(2,1)} async-done(((bf16[16,96,2048]{2,1,0:T(8,128)(2,1)}), bf16[16,96,2048]{2,1,0:T(8,128)(2,1)}, u32[]{:S(2)}, u32[]{:S(2)}) %all-to-all-start.3) | async-done | bytes 6291488 | tf_op jit(solution)/shard_map/all_to_all | solution.py:70
  381.9 8.8 %gather_fusion.3 = bf16[512,2048]{1,0:T(8,128)(2,1)} fusion(bf16[1536,2048]{1,0:T(8,128)(2,1)} %bitcast.11, s32[1024]{0:T(1024)S(1)} %pad_clamp_fusion.2), kind=kCustom, calls=%fused_computation.3 | custom fusion | bytes 4196352 | tf_op jit(solution)/shard_map/gather | solution.py:86
  390.8 4.1 %reshape.143 = bf16[128,4,2048]{2,1,0:T(4,128)(2,1)} reshape(bf16[512,2048]{1,0:T(8,128)(2,1)} %gather_fusion.3) | data formatting | bytes 4194304 | tf_op jit(solution)/shard_map/reshape | solution.py:86
  394.9 5.0 %reduce_sum.34 = bf16[128,2048]{1,0:T(8,128)(2,1)} reduce(bf16[128,4,2048]{2,1,0:T(4,128)(2,1)} %reshape.143, bf16[]{:T(256)} %constant.22.clone.1), dimensions={1}, to_apply=%region_4.5 | reduce | flops 786432 | bytes 2621442 | tf_op jit(solution)/shard_map/reduce_sum | solution.py:88
  (25 shorter events, 0.3 us)
Async XLA Ops:
  7.2 229.6 %copy-start = (bf16[1,2048,512]{2,1,0:T(8,128)(2,1)S(1)}, bf16[1,2048,512]{2,1,0:T(8,128)(2,1)}, u32[]{:S(2)}) copy-start(bf16[1,2048,512]{2,1,0:T(8,128)(2,1)} %param.11) | copy-start | bytes 6291460
  7.2 25.6 %copy-start.1 = (bf16[128,2048]{1,0:T(8,128)(2,1)S(1)}, bf16[128,2048]{1,0:T(8,128)(2,1)}, u32[]{:S(2)}) copy-start(bf16[128,2048]{1,0:T(8,128)(2,1)} %param.6) | copy-start | bytes 1572868
  24.4 15.6 %all-to-all-start = ((bf16[16,1,96]{2,1,0:T(2,128)(2,1)}), bf16[16,1,96]{2,1,0:T(2,128)(2,1)S(1)}, u32[]{:S(2)}, u32[]{:S(2)}) async-start(bf16[16,1,96]{2,1,0:T(2,128)(2,1)} %all_to_all.25), calls=%async_computation | async-start | bytes 16384 | tf_op jit(solution)/shard_map/all_to_all | solution.py:44
  40.0 6.8 %copy-start.2 = (bf16[128,2048]{1,0:T(8,128)(2,1)S(1)}, bf16[128,2048]{1,0:T(8,128)(2,1)}, u32[]{:S(2)}) copy-start(bf16[128,2048]{1,0:T(8,128)(2,1)} %param.7) | copy-start | bytes 1572868
  40.0 98.7 %all-to-all-start.2 = ((bf16[16,96,2048]{2,1,0:T(8,128)(2,1)}), bf16[16,96,2048]{2,1,0:T(8,128)(2,1)}, u32[]{:S(2)}, u32[]{:S(2)}) async-start(bf16[16,96,2048]{2,1,0:T(8,128)(2,1)} %bitcast.57), calls=%async_computation.2 | async-start | bytes 12582912 | tf_op jit(solution)/shard_map/all_to_all | solution.py:42
  138.6 94.1 %all-to-all-start.1 = ((bf16[16,96,2048]{2,1,0:T(8,128)(2,1)}), bf16[16,96,2048]{2,1,0:T(8,128)(2,1)}, u32[]{:S(2)}, u32[]{:S(2)}) async-start(bf16[16,96,2048]{2,1,0:T(8,128)(2,1)} %bitcast.56), calls=%async_computation.1 | async-start | bytes 12582912 | tf_op jit(solution)/shard_map/all_to_all | solution.py:43
  143.4 256.4 %reduce-scatter.5.cloned.1.call-start = ((), (), s32[]{:S(2)}) async-start(), calls=%async_computation.8 | async-start | bytes 4718592 | tf_op jit(solution)/shard_map/reduce_scatter | solution.py:98
  232.8 4.6 %copy-start.4 = (f32[1536,1024]{0,1:T(8,128)S(1)}, f32[1536,1024]{0,1:T(8,128)}, u32[]{:S(2)}) copy-start(f32[1536,1024]{0,1:T(8,128)} %fusion.4) | copy-start | bytes 18874372
  243.8 4.4 %copy-start.3 = (bf16[1536,512]{0,1:T(8,128)(2,1)}, bf16[1536,512]{0,1:T(8,128)(2,1)S(1)}, u32[]{:S(2)}) copy-start(bf16[1536,512]{0,1:T(8,128)(2,1)S(1)} %get-tuple-element.18) | copy-start | bytes 4718596
  253.8 146.1 %reduce-scatter.3.cloned.1.call-start = ((), (), s32[]{:S(2)}) async-start(), calls=%async_computation.7 | async-start | bytes 9437184 | tf_op jit(solution)/shard_map/reduce_scatter | solution.py:90
  272.8 16.8 %all-to-all-start.4 = ((bf16[16,1,96]{2,1,0:T(2,128)(2,1)}), bf16[16,1,96]{2,1,0:T(2,128)(2,1)S(1)}, u32[]{:S(2)}, u32[]{:S(2)}) async-start(bf16[16,1,96]{2,1,0:T(2,128)(2,1)} %convert_element_type.83), calls=%async_computation.4 | async-start | bytes 16384 | tf_op jit(solution)/shard_map/all_to_all | solution.py:77
  289.6 92.4 %all-to-all-start.3 = ((bf16[16,96,2048]{2,1,0:T(8,128)(2,1)}), bf16[16,96,2048]{2,1,0:T(8,128)(2,1)}, u32[]{:S(2)}, u32[]{:S(2)}) async-start(bf16[16,96,2048]{2,1,0:T(8,128)(2,1)} %bitcast.58), calls=%async_computation.3 | async-start | bytes 12582912 | tf_op jit(solution)/shard_map/all_to_all | solution.py:70
Sparse Core Ops, SparseCore 0:
  253.9 37.6 reduce-scatter.4
  294.5 53.8 reduce-scatter.2
where the time goes:
time: 411 us; the launch traced here: 407 us
  waiting for transfers between devices  243 us (59%)
  matrix products  53.2 us (13%)
  local copies, waits for them, and re-layouts  48.1 us (12%)
  starting transfers between devices  32.6 us (8%)
  other arithmetic  15.5 us (4%)
  between operations  14.3 us (3%)
    all_to_all x1, waiting for transfers between devices, body(): lax.all_to_all(send_x, 'expert', split_axis=0, concat_axis=0, tiled=True)  84.7 us
    all_to_all x1, waiting for transfers between devices, body(): lax.all_to_all(slot_grad.reshape(experts_all, capacity, feature_dim), 'ex...  81.2 us
    all_to_all x1, waiting for transfers between devices, body(): lax.all_to_all(send_g, 'expert', split_axis=0, concat_axis=0, tiled=True)  77.1 us
    gather x3, local copies, waits for them, and re-layouts, padded_rows(): return jnp.concatenate([values, zero_row], axis=0)[index]  23.6 us
    dot_general x1, matrix products, body(): pre = jnp.dot(rows_x, weight_gu, preferred_element_type=jnp.float32)  11.8 us
    dot_general x1, matrix products, body(): lax.dot_general(rows_x, pre_grad, (((0,), (0,)), ((), ())), preferred_ele...  11.8 us
    dot_general x1, matrix products, body(): lax.dot_general(pre_grad, weight_gu, (((1,), (1,)), ((), ())), preferred_...  11.4 us
    gather x1, local copies, waits for them, and re-layouts, body(): back[0].reshape(total_slots, feature_dim)[slots]  8.82 us
  transfers between devices with their start and end apart: 7, of which 3 were waited for; matrix products, arithmetic and copies ran while one was open for 19% of the time, Pallas kernels for 0%

commit v1 on v0

v1 whole, which is shorter than its diff:
```python
import jax
import jax.numpy as jnp
from jax import lax
from jax.sharding import PartitionSpec as P


def body(activations, out_grad, combine_weights, expert_ids, gate_up_weight, down_weight):
    experts_all = lax.axis_size("expert")
    me = lax.axis_index("expert")
    columns = jnp.arange(experts_all, dtype=jnp.int32)
    named = expert_ids[:, :, None] == columns[None, None, :]
    table = jnp.sum(
        jnp.where(named, combine_weights.astype(jnp.float32)[:, :, None], 0.0), axis=1
    ).astype(jnp.bfloat16)
    rows_x = lax.all_gather(activations, "expert", axis=0, tiled=True)
    rows_g = lax.all_gather(out_grad, "expert", axis=0, tiled=True)
    tables = lax.all_gather(table, "expert", axis=0, tiled=True)
    mine = (columns == me).astype(jnp.float32)
    rows_w = jnp.sum(tables.astype(jnp.float32) * mine[None, :], axis=1, keepdims=True)
    weight_gu = gate_up_weight[0]
    weight_down = down_weight[0]
    hidden_dim = weight_down.shape[1]
    pre = jnp.dot(rows_x, weight_gu, preferred_element_type=jnp.float32)
    gate = pre[:, :hidden_dim]
    upper = pre[:, hidden_dim:]
    sig = jax.nn.sigmoid(gate)
    hidden = (gate * sig * upper).astype(jnp.bfloat16).astype(jnp.float32)
    raw = jnp.dot(rows_g, weight_down, preferred_element_type=jnp.float32)
    prob = jnp.sum(hidden * raw, axis=1, keepdims=True)
    hidden_grad = raw * rows_w
    gate_grad = hidden_grad * upper * sig * (1.0 + gate * (1.0 - sig))
    upper_grad = hidden_grad * gate * sig
    pre_grad = jnp.concatenate([gate_grad, upper_grad], axis=1).astype(jnp.bfloat16)
    scaled = (hidden * rows_w).astype(jnp.bfloat16)
    slot_grad = lax.dot_general(
        pre_grad, weight_gu, (((1,), (1,)), ((), ())), preferred_element_type=jnp.float32
    ).astype(jnp.bfloat16)
    grad_input = lax.psum_scatter(slot_grad, "expert", scatter_dimension=0, tiled=True)
    probs = lax.psum_scatter(
        (prob * mine[None, :]).astype(jnp.bfloat16), "expert", scatter_dimension=0, tiled=True
    )
    grad_combine = jnp.sum(
        jnp.where(named, probs.astype(jnp.float32)[:, None, :], 0.0), axis=2
    ).astype(jnp.bfloat16)
    grad_gate_up = lax.psum_scatter(
        lax.dot_general(
            rows_x, pre_grad, (((0,), (0,)), ((), ())), preferred_element_type=jnp.float32
        ).astype(jnp.bfloat16),
        "group",
        scatter_dimension=0,
        tiled=True,
    ).astype(jnp.float32)
    grad_down = lax.psum_scatter(
        lax.dot_general(
            rows_g, scaled, (((0,), (0,)), ((), ())), preferred_element_type=jnp.float32
        ).astype(jnp.bfloat16),
        "group",
        scatter_dimension=0,
        tiled=True,
    ).astype(jnp.float32)
    return (grad_input, grad_combine, grad_gate_up[None], grad_down[None])


def solution(mesh):
    rows = P(("expert", "group"), None)
    return jax.shard_map(
        body,
        mesh=mesh,
        in_specs=(rows, rows, rows, rows, P("expert", None, None), P("expert", None, None)),
        out_specs=(rows, rows, P("expert", "group", None), P("expert", "group", None)),
        check_vma=False,
    )
```

time: 411 us -> 444 us (1.080)
  waiting for transfers between devices: 243 us -> 334 us
  local copies, waits for them, and re-layouts: 48.1 us -> 6.11 us
  starting transfers between devices: 32.6 us -> 0.42 us
  blocking collectives: 0 us -> 16.7 us
  matrix products: 53.2 us -> 63.1 us
  other arithmetic: 15.5 us -> 8.64 us
    all_to_all x5 -> x0, waiting for transfers between devices: 243 us -> none  [the longest x1 84.7 us: body(): lax.all_to_all(send_x, 'expert', split_axis=0, concat_axis=0, tiled=True)]
    all_gather x0 -> x2, waiting for transfers between devices: none -> 133 us  [the longest x1 75.4 us: body(): rows_x = lax.all_gather(activations, 'expert', axis=0, tiled=True)]
    reduce_scatter x1 -> x2, waiting for transfers between devices: 0.01 us -> 90.7 us  [the longest x1 87.8 us: body(): lax.psum_scatter(slot_grad, 'expert', scatter_dimension=0, tiled=True)]
    unnamed x2 -> x7, waiting for transfers between devices: 0.03 us -> 73.2 us
    reduce_scatter x1, waiting for transfers between devices: 0.01 us -> 37 us  [body(): lax.psum_scatter(lax.dot_general(rows_x, pre_grad, (((0,), (0,)), ((), ()...]
    gather x5 -> x0, local copies, waits for them, and re-layouts: 36 us -> none  [the longest x3 23.6 us: padded_rows(): return jnp.concatenate([values, zero_row], axis=0)[index]]
    all_to_all x5 -> x0, starting transfers between devices: 32.2 us -> none  [the longest x1 8.42 us: body(): lax.all_to_all(send_w, 'expert', split_axis=0, concat_axis=0, tiled=True)]
    all_gather x0 -> x1, blocking collectives: none -> 16.7 us  [body(): tables = lax.all_gather(table, 'expert', axis=0, tiled=True)]
  transfers between devices with their start and end apart: 7 -> 6, of which waited for: 3 -> 6; matrix products, arithmetic and copies ran while one was open for 19% -> 12% of each run, Pallas kernels for 0% -> 0%
where the time goes in v1:
time: 444 us; the launch traced here: 443 us
  waiting for transfers between devices  334 us (75%)
  matrix products  63.1 us (14%)
  blocking collectives  16.7 us (4%)
  between operations  14.2 us (3%)
  other arithmetic  8.64 us (2%)
  local copies, waits for them, and re-layouts  6.11 us (1%)
    reduce_scatter x1, waiting for transfers between devices, body(): lax.psum_scatter(slot_grad, 'expert', scatter_dimension=0, tiled=True)  87.8 us
    all_gather x1, waiting for transfers between devices, body(): rows_x = lax.all_gather(activations, 'expert', axis=0, tiled=True)  75.4 us
    unnamed x7, waiting for transfers between devices  73.2 us
    all_gather x1, waiting for transfers between devices, body(): rows_g = lax.all_gather(out_grad, 'expert', axis=0, tiled=True)  58 us
    reduce_scatter x1, waiting for transfers between devices, body(): lax.psum_scatter(lax.dot_general(rows_x, pre_grad, (((0,), (0,)), ((), ()...  37 us
    all_gather x1, blocking collectives, body(): tables = lax.all_gather(table, 'expert', axis=0, tiled=True)  16.7 us
    dot_general x1, matrix products, body(): pre = jnp.dot(rows_x, weight_gu, preferred_element_type=jnp.float32)  14.7 us
    dot_general x1, matrix products, body(): lax.dot_general(pre_grad, weight_gu, (((1,), (1,)), ((), ())), preferred_...  14 us
  transfers between devices with their start and end apart: 6, of which 6 were waited for; matrix products, arithmetic and copies ran while one was open for 12% of the time, Pallas kernels for 0%

profile of v1, /device:TPU:1, one launch (start us, length us, event | category | flops | bytes accessed | tf_op | source)
XLA Modules:
  0.0 443.4 jit_solution(17004456806041273709)
XLA Ops:
  7.2 0.0 copy-start
  7.2 0.0 all-gather.5.cloned.1.call-start
  7.2 0.7 all-gather.5.cloned.1.call-update
  7.9 0.0 all-gather.3.cloned.1.call-start
  8.0 0.7 all-gather.3.cloned.1.call-update
  8.7 0.0 reduce-scatter.13.cloned.1.call-start
  8.7 75.4 %all-gather.5.cloned.1.call-done = bf16[2048,2048]{1,0:T(8,128)(2,1)} async-done(((bf16[128,2048]{1,0:T(8,128)(2,1)}), bf16[2048,2048]{1,0:T(8,128)(2,1)}) %all-gather.5.cloned.1.call-update) | async-done | bytes 8388624 | tf_op jit(solution)/shard_map/all_gather | solution.py:15
  84.1 14.7 %fusion.3 = f32[2048,1024]{0,1:T(8,128)} fusion(bf16[2048,2048]{1,0:T(8,128)(2,1)} %all-gather.5.cloned.1.call-done, bf16[1,2048,1024]{2,1,0:T(8,128)(2,1)} %param.10), kind=kOutput, calls=%fused_computation.7 | convolution fusion | flops 8589934592 | bytes 20971520 | tf_op jit(solution)/shard_map/dot_general | solution.py:23
  98.8 0.0 copy-start.4
  98.8 0.0 copy-start.3
  98.8 58.0 %all-gather.3.cloned.1.call-done = bf16[2048,2048]{1,0:T(8,128)(2,1)} async-done(((bf16[128,2048]{1,0:T(8,128)(2,1)}), bf16[2048,2048]{1,0:T(8,128)(2,1)}) %all-gather.3.cloned.1.call-update) | async-done | bytes 8388624 | tf_op jit(solution)/shard_map/all_gather | solution.py:16
  156.8 0.0 copy-done
  156.8 11.9 %fusion = (f32[2048]{0:T(1024)S(1)}, bf16[2048,512]{0,1:T(8,128)(2,1)}, f32[2048,512]{0,1:T(8,128)}) fusion(f32[2048,1024]{0,1:T(8,128)} %fusion.3, bf16[2048,2048]{1,0:T(8,128)(2,1)} %all-gather.3.cloned.1.call-done, bf16[1,2048,512]{2,1,0:T(8,128)(2,1)S(1)} %copy-done), kind=kOutput, calls=%fused_computation.3 | convolution fusion | flops 4304402432 | bytes 25174016 | tf_op jit(solution)/shard_map/dot_general | solution.py:28
  168.7 0.1 multiply_convert_fusion.3
  168.8 1.0 copy.18
  169.8 0.0 reduce-scatter.13.cloned.1.call-update
  169.8 0.0 reduce-scatter.11.cloned.1.call-start
  169.8 0.0 copy-done.4
  169.9 71.7 %reduce-scatter.13.cloned.1.call-done = bf16[128,16]{1,0:T(8,128)(2,1)} async-done(((bf16[2048,16]{1,0:T(8,128)(2,1)}), bf16[128,16]{1,0:T(8,128)(2,1)}) %reduce-scatter.13.cloned.1.call-update) | async-done | bytes 4112
  241.6 0.8 copy.19
  242.4 0.0 copy-done.3
  242.4 0.6 select_reduce_fusion
  243.0 16.7 %all_gather.10 = bf16[2048,16]{0,1:T(8,128)(2,1)S(1)} all-gather(bf16[128,16]{0,1:T(8,128)(2,1)S(1)} %get-tuple-element.17), channel_id=1, replica_groups=mesh['expert'=16,'group'=8] {'expert'}, dimensions={0}, use_global_device_ids=true | all-gather | bytes 69632 | tf_op jit(solution)/shard_map/all_gather | solution.py:17
  259.7 0.1 multiply_reduce_fusion
  259.8 9.9 %fusion.5 = bf16[2048,512]{0,1:T(8,128)(2,1)} fusion(bf16[2048,2048]{1,0:T(8,128)(2,1)} %all-gather.3.cloned.1.call-done, bf16[2048,512]{0,1:T(8,128)(2,1)} %get-tuple-element.19, f32[2048]{0:T(1024)S(1)} %multiply_reduce_fusion), kind=kOutput, calls=%fused_computation.15 | convolution fusion | flops 4299161600 | bytes 12591104 | tf_op jit(solution)/shard_map/dot_general | solution.py:54
  269.7 0.0 reduce-scatter.11.cloned.1.call-update
  269.7 0.2 reduce-scatter.9.cloned.1.call-start
  269.9 5.7 %multiply_convert_fusion.2 = (bf16[2048,512]{0,1:T(8,128)(2,1)S(1)}, bf16[2048,512]{0,1:T(8,128)(2,1)S(1)}) fusion(f32[2048,1024]{0,1:T(8,128)} %fusion.3, f32[2048,512]{0,1:T(8,128)} %get-tuple-element.22, f32[2048]{0:T(1024)S(1)} %multiply_reduce_fusion), kind=kLoop, calls=%fused_computation.12 | loop fusion | flops 14680064 | bytes 16785408 | tf_op jit(solution)/shard_map/convert.2
  275.7 0.0 copy-start.1
  275.7 0.0 copy-start.2
  275.7 1.3 copy-done.1
  277.0 0.7 copy-done.2
  277.7 12.6 %convert_bitcast_fusion = bf16[2048,1024]{0,1:T(8,128)(2,1)} fusion(bf16[2048,2048]{1,0:T(8,128)(2,1)} %all-gather.5.cloned.1.call-done, bf16[2048,512]{0,1:T(8,128)(2,1)S(1)} %get-tuple-element.21, bf16[2048,512]{0,1:T(8,128)(2,1)S(1)} %get-tuple-element.20), kind=kOutput, calls=%fused_computation.9 | convolution fusion | flops 8600420352 | bytes 16777216 | tf_op jit(solution)/shard_map/dot_general | solution.py:46
  290.3 0.0 reduce-scatter.9.cloned.1.call-update
  290.3 0.0 reduce-scatter.7.cloned.1.call-start
  290.4 14.0 %convolution_convert_fusion = bf16[2048,2048]{1,0:T(8,128)(2,1)} fusion(bf16[1,2048,1024]{2,1,0:T(8,128)(2,1)} %param.10, bf16[2048,512]{0,1:T(8,128)(2,1)} %copy-done.2, bf16[2048,512]{0,1:T(8,128)(2,1)} %copy-done.1), kind=kOutput, calls=%fused_computation | convolution fusion | flops 8602517504 | bytes 16777216 | tf_op jit(solution)/shard_map/dot_general | solution.py:35
  304.4 0.0 reduce-scatter.7.cloned.1.call-update
  304.5 2.9 reduce-scatter.11.cloned.1.call-done
  307.3 1.0 bitcast_convert_fusion.1
  308.3 1.0 copy.17
  309.3 37.0 %reduce-scatter.9.cloned.1.call-done = bf16[256,1024]{0,1:T(8,128)(2,1)} async-done(((bf16[2048,1024]{0,1:T(8,128)(2,1)}), bf16[256,1024]{0,1:T(8,128)(2,1)}) %reduce-scatter.9.cloned.1.call-update) | async-done | bytes 524304 | tf_op jit(solution)/shard_map/reduce_scatter | solution.py:45
  346.3 1.1 bitcast_convert_fusion
  347.4 1.3 copy.16
  348.7 87.8 %reduce-scatter.7.cloned.1.call-done = bf16[128,2048]{1,0:T(8,128)(2,1)} async-done(((bf16[2048,2048]{1,0:T(8,128)(2,1)}), bf16[128,2048]{1,0:T(8,128)(2,1)}) %reduce-scatter.7.cloned.1.call-update) | async-done | bytes 524304 | tf_op jit(solution)/shard_map/reduce_scatter | solution.py:38
  (3 shorter events, 0.0 us)
Async XLA Ops:
  7.2 149.7 %copy-start = (bf16[1,2048,512]{2,1,0:T(8,128)(2,1)S(1)}, bf16[1,2048,512]{2,1,0:T(8,128)(2,1)}, u32[]{:S(2)}) copy-start(bf16[1,2048,512]{2,1,0:T(8,128)(2,1)} %param.11) | copy-start | bytes 6291460
  7.2 77.0 %all-gather.5.cloned.1.call-start = ((), (), s32[]{:S(2)}) async-start(), calls=%async_computation.5 | async-start | bytes 8912896 | tf_op jit(solution)/shard_map/all_gather | solution.py:15
  7.9 148.9 %all-gather.3.cloned.1.call-start = ((), (), s32[]{:S(2)}) async-start(), calls=%async_computation.4 | async-start | bytes 8912896 | tf_op jit(solution)/shard_map/all_gather | solution.py:16
  8.7 232.9 %reduce-scatter.13.cloned.1.call-start = ((), (), s32[]{:S(2)}) async-start(), calls=%async_computation.9 | async-start | bytes 557056
  98.8 71.1 %copy-start.4 = (bf16[128,4]{0,1:T(4,128)(2,1)S(1)}, bf16[128,4]{0,1:T(4,128)(2,1)}, u32[]{:S(2)}) copy-start(bf16[128,4]{0,1:T(4,128)(2,1)} %param.8) | copy-start | bytes 3076
  98.8 143.6 %copy-start.3 = (s32[128,4]{0,1:T(4,128)S(1)}, s32[128,4]{0,1:T(4,128)}, u32[]{:S(2)}) copy-start(s32[128,4]{0,1:T(4,128)} %param.9) | copy-start | bytes 6148
  169.8 137.6 %reduce-scatter.11.cloned.1.call-start = ((), (), s32[]{:S(2)}) async-start(), calls=%async_computation.8 | async-start | bytes 2359296 | tf_op jit(solution)/shard_map/reduce_scatter | solution.py:53
  269.7 76.6 %reduce-scatter.9.cloned.1.call-start = ((), (), s32[]{:S(2)}) async-start(), calls=%async_computation.7 | async-start | bytes 4718592 | tf_op jit(solution)/shard_map/reduce_scatter | solution.py:45
  275.7 1.3 copy-start.1
  275.7 2.0 copy-start.2
  290.3 146.2 %reduce-scatter.7.cloned.1.call-start = ((), (), s32[]{:S(2)}) async-start(), calls=%async_computation.6 | async-start | bytes 8912896 | tf_op jit(solution)/shard_map/reduce_scatter | solution.py:38
Sparse Core Ops, SparseCore 0:
  10.1 73.9 all-gather.4
  86.3 70.5 all-gather.2
  169.9 71.6 reduce-scatter.12
  269.8 37.4 reduce-scatter.10
  309.6 36.6 reduce-scatter.8
  350.2 86.3 reduce-scatter.6

commit v2 on v1

v2 whole, which is shorter than its diff:
```python
import functools

import jax
import jax.numpy as jnp
from jax import lax
from jax.experimental import pallas as pl
from jax.experimental.pallas import tpu as pltpu
from jax.sharding import PartitionSpec as P

MESH = pl.DeviceIdType.MESH
LANES = 128
ORDER = (1, 3, 2, 0)
PLACE = {offset: place for place, offset in enumerate(ORDER)}
F32 = jnp.float32
BF16 = jnp.bfloat16


def kernel(
    x_in, g_in, table_in, gu_in, down_in,
    input_out, prob_out, weight_out,
    rows, gu, down, turned, pre_grad, part,
    half_in, full_in, last_half, last_full,
    give, take, ring_half, ring_full,
    local_sem, gather_send, gather_recv, half_send, half_recv, full_send, full_recv,
    last_half_send, last_half_recv, last_full_send, last_full_recv,
    give_send, give_recv, ring_half_send, ring_half_recv, ring_full_send, ring_full_recv,
):
    tok, dim = x_in.shape
    hid = down_in.shape[1]
    half = tok // 2
    group = 4 * tok
    tile = hid // 2
    feat = dim // 8
    e, q = lax.axis_index("expert"), lax.axis_index("group")
    z, x, y, c = e // 4, e % 4, q // 2, q % 2
    a, b = (1 - c) * x + c * z, (1 - c) * z + c * x
    sa, sb = 1 + 3 * c, 4 - 3 * c

    def dev_a(step):
        return (((a + step + 4) % 4) * sa + b * sb, q)

    def dev_b(step):
        return (a * sa + ((b + step + 4) % 4) * sb, q)

    def dev_y(step):
        return (e, ((y + step + 4) % 4) * 2 + c)

    other = (e, y * 2 + 1 - c)

    def remote(src, dst, send, recv, dev):
        return pltpu.make_async_remote_copy(
            src_ref=src, dst_ref=dst, send_sem=send, recv_sem=recv, device_id=dev, device_id_type=MESH
        )

    def piece(da, db, h):
        return rows.at[pl.ds(PLACE[da] * group + db * tok + h * half, half), :]

    def pass_on(src, dst, h, dev):
        da, db = dst
        return remote(piece(*src, h), piece(da, db, h), gather_send.at[da, db, h], gather_recv.at[da, db, h], dev)

    def arrived(da, db, h):
        pass_on((da, db), (da, db), h, other).wait_recv()

    def along_b(da):
        for k in range(2):
            pass_on((da, 0), (da, 1), k, dev_b(-1)).start()
            pass_on((da, 0), (da, 3), 1 - k, dev_b(1)).start()

    def onward_b(da):
        arrived(da, 1, 0)
        pass_on((da, 1), (da, 2), 0, dev_b(-1)).start()
        arrived(da, 3, 1)
        pass_on((da, 3), (da, 2), 1, dev_b(1)).start()

    def rest_of(da):
        arrived(da, 1, 1)
        arrived(da, 3, 0)
        arrived(da, 2, 0)
        arrived(da, 2, 1)

    def share(da, db, h=None):
        start = PLACE[da] * group + db * tok
        if h is None:
            return part.at[pl.ds(start, tok), :]
        return part.at[pl.ds(start + h * half, half), :]

    def add_into(dst, *srcs):
        total = dst[...].astype(F32)
        for src in srcs:
            total = total + src[...].astype(F32)
        dst[...] = total.astype(dst.dtype)

    def half_copy(da, k):
        dev = dev_b(1) if k == 0 else dev_b(-1)
        return remote(share(da, 2, k), half_in.at[da, k], half_send.at[da, k], half_recv.at[da, k], dev)

    def full_copy(da, k):
        dev = dev_b(1) if k == 0 else dev_b(-1)
        return remote(share(da, 1 + 2 * k), full_in.at[da, k], full_send.at[da, k], full_recv.at[da, k], dev)

    def last_half_copy(k):
        dev = dev_a(1) if k == 0 else dev_a(-1)
        return remote(share(2, 0, k), last_half.at[k], last_half_send.at[k], last_half_recv.at[k], dev)

    def last_full_copy(k):
        dev = dev_a(1) if k == 0 else dev_a(-1)
        return remote(share(1 + 2 * k, 0), last_full.at[k], last_full_send.at[k], last_full_recv.at[k], dev)

    def send_halves(da):
        for k in range(2):
            half_copy(da, k).start()

    def send_fulls(da):
        for k in range(2):
            half_copy(da, k).wait_recv()
            add_into(share(da, 1 + 2 * k, k), half_in.at[da, k])
            full_copy(da, k).start()

    def settle(da):
        for k in range(2):
            full_copy(da, k).wait_recv()
        add_into(share(da, 0), full_in.at[da, 0], full_in.at[da, 1])

    def column(r0):
        table = rows[pl.ds(r0, group), pl.ds(2 * dim, LANES)].astype(F32)
        lane = lax.broadcasted_iota(jnp.int32, (group, LANES), 1)
        return jnp.sum(jnp.where(lane == e, table, 0.0), axis=1, keepdims=True)

    def forward(da):
        r0 = PLACE[da] * group
        weight = column(r0)

        def step(n, prob):
            n0 = pl.multiple_of(n * tile, tile)
            n1 = pl.multiple_of(hid + n * tile, tile)
            n2 = pl.multiple_of(2 * hid + n * tile, tile)
            xs = rows[pl.ds(r0, group), pl.ds(0, dim)]
            gate = jnp.dot(xs, gu[:, pl.ds(n0, tile)], preferred_element_type=F32)
            upper = jnp.dot(xs, gu[:, pl.ds(n1, tile)], preferred_element_type=F32)
            raw = jnp.dot(
                rows[pl.ds(r0, group), pl.ds(dim, dim)], down[:, pl.ds(n0, tile)], preferred_element_type=F32
            )
            sig = jax.nn.sigmoid(gate)
            silu = gate * sig
            hidden = (silu * upper).astype(BF16).astype(F32)
            grad = raw * weight
            gate_grad = (grad * upper * sig * (1.0 + gate * (1.0 - sig))).astype(BF16)
            upper_grad = (grad * silu).astype(BF16)
            pre_grad[:, pl.ds(n0, tile)] = gate_grad
            pre_grad[:, pl.ds(n1, tile)] = upper_grad
            turned[pl.ds(n0, tile), pl.ds(r0, group)] = gate_grad.T
            turned[pl.ds(n1, tile), pl.ds(r0, group)] = upper_grad.T
            turned[pl.ds(n2, tile), pl.ds(r0, group)] = (hidden * weight).astype(BF16).T
            return prob + jnp.sum(hidden * raw, axis=1, keepdims=True)

        prob = lax.fori_loop(0, 2, step, jnp.zeros((group, 1), F32))
        lane = lax.broadcasted_iota(jnp.int32, (group, LANES), 1)
        part[pl.ds(r0, group), pl.ds(dim, LANES)] = jnp.where(lane == e, prob, 0.0).astype(BF16)

    def backward(da):
        r0 = PLACE[da] * group
        wide = dim // 4

        @pl.loop(0, 4)
        def _(m):
            m0 = pl.multiple_of(m * wide, wide)
            part[pl.ds(r0, group), pl.ds(m0, wide)] = lax.dot_general(
                pre_grad[...], gu[pl.ds(m0, wide), :], (((1,), (1,)), ((), ())), preferred_element_type=F32
            ).astype(BF16)

    def weight_block(dy, core, put):
        f0 = (((y + dy) % 4) * 2 + core) * feat

        @pl.loop(0, 3)
        def _(i):
            i0 = pl.multiple_of(i * hid, hid)
            lane = pl.multiple_of(f0 + dim * (i // 2), feat)
            put(i0, jnp.dot(turned[pl.ds(i0, hid), :], rows[:, pl.ds(lane, feat)], preferred_element_type=F32))

    def give_copy(dy):
        return remote(give.at[dy], take.at[dy], give_send.at[dy], give_recv.at[dy], other)

    high = 3 * hid // 2

    def ring_half_copy(k):
        dev = dev_y(1) if k == 0 else dev_y(-1)
        return remote(
            take.at[2, pl.ds(k * high, high), :], ring_half.at[k], ring_half_send.at[k], ring_half_recv.at[k], dev
        )

    def ring_full_copy(k):
        dev = dev_y(1) if k == 0 else dev_y(-1)
        return remote(take.at[1 + 2 * k], ring_full.at[k], ring_full_send.at[k], ring_full_recv.at[k], dev)

    def weight_grad(dy):
        def put_give(i0, value):
            give[dy, pl.ds(i0, hid), :] = value.astype(BF16)

        weight_block(dy, 1 - c, put_give)
        give_copy(dy).start()

        def put_own(i0, value):
            weight_out[pl.ds(i0, hid), :] = value

        weight_block(dy, c, put_own)
        give_copy(dy).wait_recv()
        if dy == 0:
            weight_out[...] = weight_out[...] + take[0].astype(F32)
            return
        take[dy] = (weight_out[...] + take[dy].astype(F32)).astype(BF16)
        if dy == 2:
            for k in range(2):
                ring_half_copy(k).start()
        else:
            k = dy // 2
            ring_half_copy(k).wait_recv()
            add_into(take.at[dy, pl.ds(k * high, high), :], ring_half.at[k])
            ring_full_copy(k).start()

    own = pl.ds(PLACE[0] * group, tok)
    mine = [
        pltpu.make_async_copy(x_in, rows.at[own, pl.ds(0, dim)], local_sem.at[0]),
        pltpu.make_async_copy(g_in, rows.at[own, pl.ds(dim, dim)], local_sem.at[1]),
        pltpu.make_async_copy(table_in, rows.at[own, pl.ds(2 * dim, LANES)], local_sem.at[2]),
    ]
    weights = [
        pltpu.make_async_copy(gu_in, gu, local_sem.at[3]),
        pltpu.make_async_copy(down_in, down, local_sem.at[4]),
    ]
    for copy in mine + weights:
        copy.start()
    barrier = pltpu.get_barrier_semaphore()
    for dev in (dev_a(1), dev_a(-1), dev_b(1), dev_b(-1), dev_y(1), dev_y(-1), other):
        pl.semaphore_signal(barrier, inc=1, device_id=dev, device_id_type=MESH)
    pl.semaphore_wait(barrier, 7)
    for copy in mine:
        copy.wait()

    for k in range(2):
        pass_on((0, 0), (1, 0), k, dev_a(-1)).start()
        pass_on((0, 0), (3, 0), 1 - k, dev_a(1)).start()
    arrived(1, 0, 0)
    pass_on((1, 0), (2, 0), 0, dev_a(-1)).start()
    arrived(3, 0, 1)
    pass_on((3, 0), (2, 0), 1, dev_a(1)).start()
    arrived(1, 0, 1)
    along_b(1)
    arrived(3, 0, 0)
    onward_b(1)
    along_b(3)
    for copy in weights:
        copy.wait()

    rest_of(1)
    forward(1)
    onward_b(3)
    arrived(2, 0, 0)
    arrived(2, 0, 1)
    along_b(2)
    backward(1)
    send_halves(1)

    rest_of(3)
    forward(3)
    onward_b(2)
    along_b(0)
    send_fulls(1)
    backward(3)
    send_halves(3)

    rest_of(2)
    forward(2)
    onward_b(0)
    settle(1)
    send_fulls(3)
    backward(2)
    send_halves(2)

    rest_of(0)
    forward(0)
    settle(3)
    send_fulls(2)
    backward(0)
    send_halves(0)

    weight_grad(2)
    settle(2)
    for k in range(2):
        last_half_copy(k).start()
    send_fulls(0)
    weight_grad(1)
    for k in range(2):
        last_half_copy(k).wait_recv()
        add_into(share(1 + 2 * k, 0, k), last_half.at[k])
        last_full_copy(k).start()
    weight_grad(3)
    settle(0)
    weight_grad(0)
    for k in range(2):
        last_full_copy(k).wait_recv()
    add_into(share(0, 0), last_full.at[0], last_full.at[1])
    input_out[...] = part[own, pl.ds(0, dim)]
    prob_out[...] = part[own, pl.ds(dim, LANES)]
    for k in range(2):
        ring_full_copy(k).wait_recv()
    weight_out[...] = weight_out[...] + ring_full[0].astype(F32) + ring_full[1].astype(F32)

    for da in range(4):
        for db in range(4):
            if da + db > 0:
                for h in range(2):
                    pass_on((da, db), (da, db), h, other).wait_send()
        give_copy(da).wait_send()
        for k in range(2):
            half_copy(da, k).wait_send()
            full_copy(da, k).wait_send()
    for k in range(2):
        last_half_copy(k).wait_send()
        last_full_copy(k).wait_send()
        ring_half_copy(k).wait_send()
        ring_full_copy(k).wait_send()


def body(activations, out_grad, combine_weights, expert_ids, gate_up_weight, down_weight):
    tok, dim = activations.shape
    hid = down_weight.shape[2]
    columns = jnp.arange(LANES, dtype=jnp.int32)
    named = expert_ids[:, :, None] == columns[None, None, :]
    table = jnp.sum(
        jnp.where(named, combine_weights.astype(F32)[:, :, None], 0.0), axis=1
    ).astype(BF16)
    feat = dim // 8
    dma = pltpu.SemaphoreType.DMA
    vmem = pltpu.VMEM
    wide = dim + LANES
    grad_input, probs, turned = pl.pallas_call(
        kernel,
        out_shape=(
            jax.ShapeDtypeStruct((tok, dim), BF16),
            jax.ShapeDtypeStruct((tok, LANES), BF16),
            jax.ShapeDtypeStruct((3 * hid, feat), F32),
        ),
        in_specs=[pl.BlockSpec(memory_space=pl.ANY)] * 5,
        out_specs=[pl.BlockSpec(memory_space=pltpu.VMEM)] * 3,
        scratch_shapes=[
            vmem((16 * tok, 2 * dim + LANES), BF16),
            vmem((dim, 2 * hid), BF16),
            vmem((dim, hid), BF16),
            vmem((3 * hid, 16 * tok), BF16),
            vmem((4 * tok, 2 * hid), BF16),
            vmem((16 * tok, wide), BF16),
            vmem((4, 2, tok // 2, wide), BF16),
            vmem((4, 2, tok, wide), BF16),
            vmem((2, tok // 2, wide), BF16),
            vmem((2, tok, wide), BF16),
            vmem((4, 3 * hid, feat), BF16),
            vmem((4, 3 * hid, feat), BF16),
            vmem((2, 3 * hid // 2, feat), BF16),
            vmem((2, 3 * hid, feat), BF16),
            dma((5,)),
            dma((4, 4, 2)), dma((4, 4, 2)),
            dma((4, 2)), dma((4, 2)), dma((4, 2)), dma((4, 2)),
            dma((2,)), dma((2,)), dma((2,)), dma((2,)),
            dma((4,)), dma((4,)), dma((2,)), dma((2,)), dma((2,)), dma((2,)),
        ],
        compiler_params=pltpu.CompilerParams(
            collective_id=0, has_side_effects=True, vmem_limit_bytes=67043328
        ),
        name="routed",
    )(activations, out_grad, table, gate_up_weight[0], down_weight[0])
    grad_combine = jnp.sum(
        jnp.where(named, probs.astype(F32)[:, None, :], 0.0), axis=2
    ).astype(BF16)
    return (grad_input, grad_combine, turned[: 2 * hid].T[None], turned[2 * hid :].T[None])


def solution(mesh):
    rows = P(("expert", "group"), None)
    return jax.shard_map(
        body,
        mesh=mesh,
        in_specs=(rows, rows, rows, rows, P("expert", None, None), P("expert", None, None)),
        out_specs=(rows, rows, P("expert", "group", None), P("expert", "group", None)),
        check_vma=False,
    )
```

time: 444 us -> 173 us (0.39)
  waiting for transfers between devices: 334 us -> 0 us
  Pallas kernels: 0 us -> 161 us
  matrix products: 63.1 us -> 0 us
  blocking collectives: 16.7 us -> 0 us
  between operations: 14.2 us -> 0.66 us
    pallas_call x0 -> x1, Pallas kernels: none -> 161 us  [body(): pl.pallas_call(kernel, out_shape=(jax.ShapeDtypeStruct((tok, dim), BF16),...]
    all_gather x2 -> x0, waiting for transfers between devices: 133 us -> none  [the longest x1 75.4 us: body(): rows_x = lax.all_gather(activations, 'expert', axis=0, tiled=True)]
    reduce_scatter x3 -> x0, waiting for transfers between devices: 128 us -> none  [the longest x1 87.8 us: body(): lax.psum_scatter(slot_grad, 'expert', scatter_dimension=0, tiled=True)]
    unnamed x7 -> x0, waiting for transfers between devices: 73.2 us -> none
    dot_general x5 -> x0, matrix products: 63.1 us -> none  [the longest x1 14.7 us: body(): pre = jnp.dot(rows_x, weight_gu, preferred_element_type=jnp.float32)]
    all_gather x1 -> x0, blocking collectives: 16.7 us -> none  [body(): tables = lax.all_gather(table, 'expert', axis=0, tiled=True)]
    another operation x1 -> x0, other arithmetic: 5.75 us -> none
  transfers between devices with their start and end apart: 6 -> 0, of which waited for: 6 -> 0; matrix products, arithmetic and copies ran while one was open for 12% -> 0% of each run, Pallas kernels for 0% -> 0%
where the time goes in v2:
time: 173 us; the launch traced here: 172 us
  Pallas kernels  161 us (93%)
  local copies, waits for them, and re-layouts  5.47 us (3%)
  other arithmetic  4.45 us (3%)
    pallas_call x1, Pallas kernels, body(): pl.pallas_call(kernel, out_shape=(jax.ShapeDtypeStruct((tok, dim), BF16),...  161 us

profile of v2, /device:TPU:1, one launch (start us, length us, event | category | flops | bytes accessed | tf_op | source)
XLA Modules:
  0.0 171.8 jit_solution(622193601145341373)
XLA Ops:
  0.6 0.7 convert_element_type.12
  1.3 1.5 select_reduce_fusion.1.table_in
  2.8 161.2 %routed.1 = (bf16[128,2048]{1,0:T(8,128)(2,1)}, bf16[128,128]{1,0:T(8,128)(2,1)}, f32[1536,256]{1,0:T(8,128)}) custom-call(bf16[128,2048]{1,0:T(8,128)(2,1)} %x_in.1, bf16[128,2048]{1,0:T(8,128)(2,1)} %g_in.1, bf16[128,128]{1,0:T(8,128)(2,1)} %select_reduce_fusion.1.table_in, bf16[2048,1024]{1,0:T(8,128)(2,1)} %bitcast.10, bf16[2048,512]{1,0:T(8,128)(2,1)} %bitcast.11), custom_call_target="tpu_custom_call" | custom-call | tf_op jit(solution)/shard_map/routed/pallas_call | solution.py:337
  164.1 0.8 convert_element_type.14
  164.8 1.5 select_reduce_fusion
  166.3 1.1 slice_bitcast_fusion.1
  167.4 1.3 slice_bitcast_fusion
  168.7 0.0 copy-start
  168.7 1.3 copy.14
  170.0 1.0 copy.15
  171.0 0.0 copy-done
  171.0 0.8 copy.17
Async XLA Ops:
  168.7 2.3 %copy-start = (bf16[128,2048]{1,0:T(8,128)(2,1)S(1)}, bf16[128,2048]{1,0:T(8,128)(2,1)}, u32[]{:S(2)}) copy-start(bf16[128,2048]{1,0:T(8,128)(2,1)} %get-tuple-element.22) | copy-start | bytes 1572868

commit v3 on v1

v3 whole, which is shorter than its diff:
```python
import functools

import jax
import jax.numpy as jnp
from jax import lax
from jax.experimental import pallas as pl
from jax.experimental.pallas import tpu as pltpu
from jax.sharding import PartitionSpec as P

MESH = pl.DeviceIdType.MESH
LANES = 128
PLACE = {0: 0, 1: 1, 3: 2, 2: 3}
F32 = jnp.float32
BF16 = jnp.bfloat16


def kernel(
    x_in, g_in, ids_in, scale_in, gu_in, down_in,
    input_out, combine_out, gu_out, down_out,
    rows, weights, turned, pre_grad, part,
    cross_in, quarter_in, full_in, back_in,
    give, take, ring_half, ring_full, paired, block,
    local_sem, gather_send, gather_recv, weight_send, weight_recv,
    cross_send, cross_recv, quarter_send, quarter_recv, full_send, full_recv, back_send, back_recv,
    give_send, give_recv, ring_half_send, ring_half_recv, ring_full_send, ring_full_recv, pair_send, pair_recv,
):
    tok, dim = x_in.shape
    hid = down_in.shape[1]
    half, quarter = tok // 2, tok // 4
    tile = hid // 2
    feat = dim // 8
    e, q = lax.axis_index("expert"), lax.axis_index("group")
    z, x, y, c = e // 4, e % 4, q // 2, q % 2
    mate = (z + 1 - 2 * (z % 2)) * 4 + x
    expert = (e, mate)

    def dev_x(step):
        return (z * 4 + (x + step + 4) % 4, q)

    def dev_y(step):
        return (e, ((y + step + 4) % 4) * 2 + c)

    across = ((3 - z) * 4 + x, q)
    pair = (mate, q)
    other = (e, y * 2 + 1 - c)

    def remote(src, dst, send, recv, dev):
        return pltpu.make_async_remote_copy(
            src_ref=src, dst_ref=dst, send_sem=send, recv_sem=recv, device_id=dev, device_id_type=MESH
        )

    def place(zz, dx, h, s=None):
        start = PLACE[dx] * 2 * tok + zz * tok + h * half
        return pl.ds(start, half) if s is None else pl.ds(start + s * quarter, quarter)

    def token(src, dst, h, s, dev):
        k = 0 if s is None else s
        return remote(
            rows.at[place(*src, h, s), :], rows.at[place(*dst, h, s), :],
            gather_send.at[dst[0], dst[1], h, k], gather_recv.at[dst[0], dst[1], h, k], dev,
        )

    def arrived(zz, dx, h, s=None):
        token((zz, dx), (zz, dx), h, s, other).wait_recv()

    def along(zz, h):
        token((zz, 0), (zz, 1), h, None, dev_x(-1)).start()
        token((zz, 0), (zz, 3), h, None, dev_x(1)).start()

    def onward(zz, dx, h):
        s = dx // 2
        token((zz, dx), (zz, 2), h, s, dev_x(1 if s else -1)).start()

    def over(dx, h):
        token((0, dx), (1, dx), h, None, across).start()

    def weight_rows(dy, near, p):
        core = c if near == 0 else 1 - c
        start = (((y + dy) % 4) * 2 + core) * feat + p * (feat // 2)
        return pl.ds(pl.multiple_of(start, feat // 2), feat // 2)

    def weight(dy, dst, p, dev, origin=1):
        where = weight_rows(dy, 0, p)
        return remote(
            weights.at[origin, where, :], weights.at[1, where, :],
            weight_send.at[dst[0], dst[1], p], weight_recv.at[dst[0], dst[1], p], dev,
        )

    def weight_arrived(dy, near, p):
        where = weight_rows(dy, near, p)
        remote(
            weights.at[1, where, :], weights.at[1, where, :],
            weight_send.at[dy, near, p], weight_recv.at[dy, near, p], other,
        ).wait_recv()

    def weights_first():
        weight_arrived(0, 0, 0)
        weight(0, (1, 0), 0, dev_y(-1)).start()
        weight_arrived(0, 0, 1)
        weight(0, (3, 0), 1, dev_y(1)).start()
        weight(0, (1, 0), 1, dev_y(-1)).start()
        weight(0, (3, 0), 0, dev_y(1)).start()
        for p in range(2):
            weight(0, (0, 1), p, other).start()

    def weights_second():
        weight_arrived(1, 0, 0)
        weight(1, (2, 0), 0, dev_y(-1)).start()
        weight_arrived(3, 0, 1)
        weight(3, (2, 0), 1, dev_y(1)).start()
        weight(1, (1, 1), 0, other).start()
        weight(3, (3, 1), 1, other).start()

    def weights_third():
        weight_arrived(1, 0, 1)
        weight(1, (1, 1), 1, other).start()
        weight_arrived(3, 0, 0)
        weight(3, (3, 1), 0, other).start()
        for p in range(2):
            weight_arrived(2, 0, p)
            weight(2, (2, 1), p, other).start()

    def weights_last():
        for dy in range(4):
            for p in range(2):
                weight_arrived(dy, 1, p)

    STREAMS = ((0, 1), (0, 0), (1, 0))

    def add_into(dst, *srcs):
        total = dst[...].astype(F32)
        for src in srcs:
            total = total + src[...].astype(F32)
        dst[...] = total.astype(dst.dtype)

    def cross_copy(dx):
        return remote(
            part.at[place(1, dx, 1), :], cross_in.at[PLACE[dx]], cross_send.at[dx], cross_recv.at[dx], across
        )

    def quarter_copy(n, s):
        zz, h = STREAMS[n]
        return remote(
            part.at[place(zz, 2, h, s), :], quarter_in.at[n, s],
            quarter_send.at[n, s], quarter_recv.at[n, s], dev_x(-1 if s else 1),
        )

    def full_copy(n, s):
        zz, h = STREAMS[n]
        return remote(
            part.at[place(zz, 3 if s else 1, h), :], full_in.at[n, s],
            full_send.at[n, s], full_recv.at[n, s], dev_x(-1 if s else 1),
        )

    def back_copy():
        return remote(part.at[place(1, 0, 0), :], back_in, back_send.at[0], back_recv.at[0], across)

    def crossed(dx):
        cross_copy(dx).wait_recv()
        add_into(part.at[place(0, dx, 1), :], cross_in.at[PLACE[dx]])

    def send_quarters(n):
        for s in range(2):
            quarter_copy(n, s).start()

    def send_fulls(n):
        zz, h = STREAMS[n]
        for s in range(2):
            quarter_copy(n, s).wait_recv()
            add_into(part.at[place(zz, 3 if s else 1, h, s), :], quarter_in.at[n, s])
            full_copy(n, s).start()

    def settle(n):
        zz, h = STREAMS[n]
        for s in range(2):
            full_copy(n, s).wait_recv()
        add_into(part.at[place(zz, 0, h), :], full_in.at[n, 0], full_in.at[n, 1])

    def forward(k, r0, count):
        lane = lax.broadcasted_iota(jnp.int32, (count, LANES), 1)
        table = rows[pl.ds(r0, count), pl.ds(2 * dim, LANES)].astype(F32)
        scale = jnp.sum(jnp.where(lane == expert[k], table, 0.0), axis=1, keepdims=True)

        def step(n, prob):
            n0 = pl.multiple_of(n * tile, tile)
            n1 = pl.multiple_of(hid + n * tile, tile)
            n2 = pl.multiple_of(2 * hid + n * tile, tile)
            xs = rows[pl.ds(r0, count), pl.ds(0, dim)]
            gate = jnp.dot(xs, weights[k, :, pl.ds(n0, tile)], preferred_element_type=F32)
            upper = jnp.dot(xs, weights[k, :, pl.ds(n1, tile)], preferred_element_type=F32)
            raw = jnp.dot(
                rows[pl.ds(r0, count), pl.ds(dim, dim)], weights[k, :, pl.ds(n2, tile)], preferred_element_type=F32
            )
            sig = jax.nn.sigmoid(gate)
            silu = gate * sig
            hidden = (silu * upper).astype(BF16).astype(F32)
            grad = raw * scale
            gate_grad = (grad * upper * sig * (1.0 + gate * (1.0 - sig))).astype(BF16)
            upper_grad = (grad * silu).astype(BF16)
            pre_grad[k, pl.ds(r0, count), pl.ds(n0, tile)] = gate_grad
            pre_grad[k, pl.ds(r0, count), pl.ds(n1, tile)] = upper_grad
            turned[k, pl.ds(n0, tile), pl.ds(r0, count)] = gate_grad.T
            turned[k, pl.ds(n1, tile), pl.ds(r0, count)] = upper_grad.T
            turned[k, pl.ds(n2, tile), pl.ds(r0, count)] = (hidden * scale).astype(BF16).T
            return prob + jnp.sum(hidden * raw, axis=1, keepdims=True)

        prob = lax.fori_loop(0, 2, step, jnp.zeros((count, 1), F32))
        mine = jnp.where(lane == expert[k], prob, 0.0).astype(BF16)
        if k == 0:
            part[pl.ds(r0, count), pl.ds(dim, LANES)] = mine
        else:
            part[pl.ds(r0, count), pl.ds(dim, LANES)] = part[pl.ds(r0, count), pl.ds(dim, LANES)] + mine

    def backward(r0, count):
        wide = dim // 4

        @pl.loop(0, 4)
        def _(m):
            m0 = pl.multiple_of(m * wide, wide)
            total = None
            for k in range(2):
                term = lax.dot_general(
                    pre_grad[k, pl.ds(r0, count), :], weights[k, pl.ds(m0, wide), pl.ds(0, 2 * hid)],
                    (((1,), (1,)), ((), ())), preferred_element_type=F32,
                )
                total = term if total is None else total + term
            part[pl.ds(r0, count), pl.ds(m0, wide)] = total.astype(BF16)

    def weight_block(k, dy, core, put):
        f0 = (((y + dy) % 4) * 2 + core) * feat

        @pl.loop(0, 3)
        def _(i):
            i0 = pl.multiple_of(i * hid, hid)
            lane = pl.multiple_of(f0 + dim * (i // 2), feat)
            put(i0, jnp.dot(turned[k, pl.ds(i0, hid), :], rows[:, pl.ds(lane, feat)], preferred_element_type=F32))

    def give_copy(k, dy):
        return remote(give.at[k, dy], take.at[k, dy], give_send.at[k, dy], give_recv.at[k, dy], other)

    high = 3 * hid // 2

    def ring_half_copy(k, s):
        return remote(
            take.at[k, 2, pl.ds(s * high, high), :], ring_half.at[k, s],
            ring_half_send.at[k, s], ring_half_recv.at[k, s], dev_y(-1 if s else 1),
        )

    def ring_full_copy(k, s):
        return remote(
            take.at[k, 3 if s else 1], ring_full.at[k, s],
            ring_full_send.at[k, s], ring_full_recv.at[k, s], dev_y(-1 if s else 1),
        )

    def pair_copy():
        return remote(take.at[1, 0], paired, pair_send.at[0], pair_recv.at[0], pair)

    def weight_grad(k, dy):
        def put_give(i0, value):
            give[k, dy, pl.ds(i0, hid), :] = value.astype(BF16)

        weight_block(k, dy, 1 - c, put_give)
        give_copy(k, dy).start()

        def put_own(i0, value):
            block[pl.ds(i0, hid), :] = value

        weight_block(k, dy, c, put_own)
        give_copy(k, dy).wait_recv()
        if k == 0 and dy == 0:
            block[...] = block[...] + take[0, 0].astype(F32)
            return
        take[k, dy] = (block[...] + take[k, dy].astype(F32)).astype(BF16)
        if dy == 2:
            for s in range(2):
                ring_half_copy(k, s).start()
        elif dy != 0:
            s = dy // 2
            ring_half_copy(k, s).wait_recv()
            add_into(take.at[k, dy, pl.ds(s * high, high), :], ring_half.at[k, s])
            ring_full_copy(k, s).start()

    own = pl.ds(0, tok)
    mine = [
        pltpu.make_async_copy(x_in, rows.at[own, pl.ds(0, dim)], local_sem.at[0]),
        pltpu.make_async_copy(g_in, rows.at[own, pl.ds(dim, dim)], local_sem.at[1]),
    ]
    loads = [
        pltpu.make_async_copy(gu_in, weights.at[0, :, pl.ds(0, 2 * hid)], local_sem.at[2]),
        pltpu.make_async_copy(down_in, weights.at[0, :, pl.ds(2 * hid, hid)], local_sem.at[3]),
    ]
    for copy in mine + loads:
        copy.start()
    barrier = pltpu.get_barrier_semaphore()
    for dev in (dev_x(1), dev_x(-1), dev_y(1), dev_y(-1), across, pair, other):
        pl.semaphore_signal(barrier, inc=1, device_id=dev, device_id_type=MESH)
    lanes = lax.broadcasted_iota(jnp.int32, (tok, LANES), 1)
    table = jnp.zeros((tok, LANES), F32)
    for k in range(ids_in.shape[1]):
        table = table + jnp.where(lanes == ids_in[:, k : k + 1], scale_in[:, k : k + 1].astype(F32), 0.0)
    rows[own, pl.ds(2 * dim, LANES)] = table.astype(BF16)
    pl.semaphore_wait(barrier, 7)
    for copy in mine:
        copy.wait()

    along(0, 1)
    over(0, 0)
    along(0, 0)
    over(0, 1)
    for copy in loads:
        copy.wait()
    for p in range(2):
        weight(0, (0, 0), p, pair, origin=0).start()
    for dx in (1, 3):
        arrived(0, dx, 1)
        onward(0, dx, 1)
        over(dx, 1)
    arrived(1, 0, 0)
    along(1, 0)
    weights_first()
    for dx in (1, 3):
        arrived(0, dx, 0)
        onward(0, dx, 0)
    arrived(0, 2, 1, 0)
    arrived(0, 2, 1, 1)
    over(2, 1)
    weights_second()
    for dx in (1, 3):
        arrived(1, dx, 0)
        onward(1, dx, 0)
    arrived(1, 0, 1)
    arrived(1, 1, 1)

    two = 2 * tok
    forward(0, 0, 2 * two)
    weights_third()
    arrived(1, 3, 1)
    forward(0, 2 * two, two)
    weights_last()
    forward(1, 0, 2 * two)
    forward(1, 2 * two, two)
    arrived(1, 2, 1)
    for s in range(2):
        arrived(0, 2, 0, s)
        arrived(1, 2, 0, s)
    for k in range(2):
        forward(k, 3 * two, two)

    weight_grad(1, 2)
    backward(3 * two, two)
    cross_copy(2).start()
    send_quarters(1)
    send_quarters(2)
    weight_grad(1, 1)
    backward(2 * two, two)
    cross_copy(3).start()
    crossed(2)
    send_quarters(0)
    weight_grad(1, 3)
    backward(0, 2 * two)
    cross_copy(1).start()
    cross_copy(0).start()
    send_fulls(2)
    send_fulls(1)
    weight_grad(1, 0)
    crossed(3)
    crossed(1)
    send_fulls(0)
    settle(2)
    back_copy().start()
    weight_grad(0, 2)
    weight_grad(0, 1)
    settle(1)
    weight_grad(0, 3)
    for s in range(2):
        ring_full_copy(1, s).wait_recv()
    add_into(take.at[1, 0], ring_full.at[1, 0], ring_full.at[1, 1])
    pair_copy().start()
    crossed(0)
    settle(0)
    weight_grad(0, 0)
    back_copy().wait_recv()
    add_into(part.at[place(0, 0, 0), :], back_in)
    input_out[...] = part[own, pl.ds(0, dim)]
    probs = part[own, pl.ds(dim, LANES)].astype(F32)
    for k in range(ids_in.shape[1]):
        picked = jnp.where(lanes == ids_in[:, k : k + 1], probs, 0.0)
        combine_out[:, k : k + 1] = jnp.sum(picked, axis=1, keepdims=True).astype(BF16)
    for s in range(2):
        ring_full_copy(0, s).wait_recv()
    pair_copy().wait_recv()
    total = block[...] + ring_full[0, 0].astype(F32) + ring_full[0, 1].astype(F32) + paired[...].astype(F32)
    gu_out[...] = total[: 2 * hid]
    down_out[...] = total[2 * hid :]

    sent = [(1, 0, 0, None), (1, 0, 1, None), (1, 1, 0, None), (1, 3, 0, None)]
    sent += [(0, dx, h, None) for dx in (1, 3) for h in range(2)]
    sent += [(1, dx, 1, None) for dx in (1, 2, 3)]
    sent += [(zz, 2, h, s) for zz, h in STREAMS for s in range(2)]
    for zz, dx, h, s in sent:
        token((zz, dx), (zz, dx), h, s, other).wait_send()
    for dy in range(4):
        for near in range(2):
            for p in range(2):
                weight(0, (dy, near), p, other).wait_send()
        cross_copy(dy).wait_send()
        for k in range(2):
            give_copy(k, dy).wait_send()
    for s in range(2):
        for n in range(3):
            quarter_copy(n, s).wait_send()
            full_copy(n, s).wait_send()
        for k in range(2):
            ring_half_copy(k, s).wait_send()
            ring_full_copy(k, s).wait_send()
    back_copy().wait_send()
    pair_copy().wait_send()


def body(activations, out_grad, combine_weights, expert_ids, gate_up_weight, down_weight):
    tok, dim = activations.shape
    top = expert_ids.shape[1]
    hid = down_weight.shape[2]
    feat = dim // 8
    dma = pltpu.SemaphoreType.DMA
    vmem = pltpu.VMEM
    wide = dim + LANES
    whole = pl.BlockSpec(memory_space=pltpu.VMEM)
    far = pl.BlockSpec(memory_space=pl.ANY)
    grad_input, grad_combine, grad_gu, grad_down = pl.pallas_call(
        kernel,
        out_shape=(
            jax.ShapeDtypeStruct((tok, dim), BF16),
            jax.ShapeDtypeStruct((tok, top), BF16),
            jax.ShapeDtypeStruct((2 * hid, feat), F32),
            jax.ShapeDtypeStruct((hid, feat), F32),
        ),
        in_specs=[far, far, whole, whole, far, far],
        out_specs=[whole] * 4,
        scratch_shapes=[
            vmem((8 * tok, 2 * dim + LANES), BF16),
            vmem((2, dim, 3 * hid), BF16),
            vmem((2, 3 * hid, 8 * tok), BF16),
            vmem((2, 8 * tok, 2 * hid), BF16),
            vmem((8 * tok, wide), BF16),
            vmem((4, tok // 2, wide), BF16),
            vmem((3, 2, tok // 4, wide), BF16),
            vmem((3, 2, tok // 2, wide), BF16),
            vmem((tok // 2, wide), BF16),
            vmem((2, 4, 3 * hid, feat), BF16),
            vmem((2, 4, 3 * hid, feat), BF16),
            vmem((2, 2, 3 * hid // 2, feat), BF16),
            vmem((2, 2, 3 * hid, feat), BF16),
            vmem((3 * hid, feat), BF16),
            vmem((3 * hid, feat), F32),
            dma((4,)),
            dma((2, 4, 2, 2)), dma((2, 4, 2, 2)),
            dma((4, 2, 2)), dma((4, 2, 2)),
            dma((4,)), dma((4,)), dma((3, 2)), dma((3, 2)), dma((3, 2)), dma((3, 2)), dma((1,)), dma((1,)),
            dma((2, 4)), dma((2, 4)), dma((2, 2)), dma((2, 2)), dma((2, 2)), dma((2, 2)), dma((1,)), dma((1,)),
        ],
        compiler_params=pltpu.CompilerParams(
            collective_id=0, has_side_effects=True, vmem_limit_bytes=67043328
        ),
        name="routed",
    )(activations, out_grad, expert_ids, combine_weights, gate_up_weight[0], down_weight[0])
    return (grad_input, grad_combine, grad_gu.T[None], grad_down.T[None])


def solution(mesh):
    rows = P(("expert", "group"), None)
    return jax.shard_map(
        body,
        mesh=mesh,
        in_specs=(rows, rows, rows, rows, P("expert", None, None), P("expert", None, None)),
        out_specs=(rows, rows, P("expert", "group", None), P("expert", "group", None)),
        check_vma=False,
    )
```

time: 444 us -> 160 us (0.36)
  waiting for transfers between devices: 334 us -> 0 us
  Pallas kernels: 0 us -> 148 us
  matrix products: 63.1 us -> 0 us
  blocking collectives: 16.7 us -> 0 us
  between operations: 14.2 us -> 0.64 us
  other arithmetic: 8.64 us -> 0 us
  local copies, waits for them, and re-layouts: 6.11 us -> 10.7 us
    pallas_call x0 -> x1, Pallas kernels: none -> 148 us  [body(): pl.pallas_call(kernel, out_shape=(jax.ShapeDtypeStruct((tok, dim), BF16),...]
    all_gather x2 -> x0, waiting for transfers between devices: 133 us -> none  [the longest x1 75.4 us: body(): rows_x = lax.all_gather(activations, 'expert', axis=0, tiled=True)]
    reduce_scatter x3 -> x0, waiting for transfers between devices: 128 us -> none  [the longest x1 87.8 us: body(): lax.psum_scatter(slot_grad, 'expert', scatter_dimension=0, tiled=True)]
    unnamed x7 -> x0, waiting for transfers between devices: 73.2 us -> none
    dot_general x5 -> x0, matrix products: 63.1 us -> none  [the longest x1 14.7 us: body(): pre = jnp.dot(rows_x, weight_gu, preferred_element_type=jnp.float32)]
    all_gather x1 -> x0, blocking collectives: 16.7 us -> none  [body(): tables = lax.all_gather(table, 'expert', axis=0, tiled=True)]
    another operation x1 -> x0, other arithmetic: 5.75 us -> none
    unnamed x14 -> x6, local copies, waits for them, and re-layouts: 6.11 us -> 10.7 us
  transfers between devices with their start and end apart: 6 -> 0, of which waited for: 6 -> 0; matrix products, arithmetic and copies ran while one was open for 12% -> 0% of each run, Pallas kernels for 0% -> 0%
where the time goes in v3:
time: 160 us; the launch traced here: 159 us
  Pallas kernels  148 us (92%)
  local copies, waits for them, and re-layouts  10.7 us (7%)
    pallas_call x1, Pallas kernels, body(): pl.pallas_call(kernel, out_shape=(jax.ShapeDtypeStruct((tok, dim), BF16),...  148 us
    unnamed x6, local copies, waits for them, and re-layouts  10.7 us

profile of v3, /device:TPU:1, one launch (start us, length us, event | category | flops | bytes accessed | tf_op | source)
XLA Modules:
  0.0 159.4 jit_solution(7330770161684332789)
XLA Ops:
  0.6 1.4 copy.11.scale_in
  2.0 1.4 copy.10.ids_in
  3.5 148.1 %routed.1 = (bf16[128,2048]{1,0:T(8,128)(2,1)}, bf16[128,4]{1,0:T(8,128)(2,1)}, f32[1024,256]{1,0:T(8,128)}, f32[512,256]{1,0:T(8,128)}) custom-call(bf16[128,2048]{1,0:T(8,128)(2,1)} %x_in.1, bf16[128,2048]{1,0:T(8,128)(2,1)} %g_in.1, s32[128,4]{1,0:T(8,128)} %copy.10.ids_in, bf16[128,4]{1,0:T(8,128)(2,1)} %copy.11.scale_in, bf16[2048,1024]{1,0:T(8,128)(2,1)} %bitcast.8, ...), custom_call_target="tpu_custom_call" | custom-call | tf_op jit(solution)/shard_map/routed/pallas_call | solution.py:430
  151.6 1.4 copy.12
  153.0 2.0 %copy.14 = f32[1,256,512]{2,1,0:T(8,128)} copy(f32[1,256,512]{1,2,0:T(8,128)} %bitcast.11) | data formatting | bytes 1048576
  155.0 2.5 %copy.13 = f32[1,256,1024]{2,1,0:T(8,128)} copy(f32[1,256,1024]{1,2,0:T(8,128)} %bitcast.10) | data formatting | bytes 2097152
  157.5 1.9 %copy.16 = bf16[128,2048]{1,0:T(8,128)(2,1)} copy(bf16[128,2048]{1,0:T(8,128)(2,1)} %get-tuple-element.20) | data formatting | bytes 1048576

commit v4 on v3

--- a/solution.py
+++ b/solution.py
@@ -19,10 +19,11 @@
     input_out, combine_out, gu_out, down_out,
     rows, weights, turned, pre_grad, part,
     cross_in, quarter_in, full_in, back_in,
-    give, take, ring_half, ring_full, paired, block,
+    give, take, ring_half, ring_full, early, paired, block,
     local_sem, gather_send, gather_recv, weight_send, weight_recv,
     cross_send, cross_recv, quarter_send, quarter_recv, full_send, full_recv, back_send, back_recv,
-    give_send, give_recv, ring_half_send, ring_half_recv, ring_full_send, ring_full_recv, pair_send, pair_recv,
+    give_send, give_recv, ring_half_send, ring_half_recv, ring_full_send, ring_full_recv,
+    early_send, early_recv, pair_send, pair_recv,
 ):
     tok, dim = x_in.shape
     hid = down_in.shape[1]
@@ -240,45 +241,46 @@
 
     high = 3 * hid // 2
 
-    def ring_half_copy(k, s):
-        return remote(
-            take.at[k, 2, pl.ds(s * high, high), :], ring_half.at[k, s],
-            ring_half_send.at[k, s], ring_half_recv.at[k, s], dev_y(-1 if s else 1),
-        )
-
-    def ring_full_copy(k, s):
-        return remote(
-            take.at[k, 3 if s else 1], ring_full.at[k, s],
-            ring_full_send.at[k, s], ring_full_recv.at[k, s], dev_y(-1 if s else 1),
-        )
-
-    def pair_copy():
-        return remote(take.at[1, 0], paired, pair_send.at[0], pair_recv.at[0], pair)
-
-    def weight_grad(k, dy):
-        def put_give(i0, value):
+    def part_of(k, dy, s):
+        return take.at[k, dy, pl.ds(s * high, high), :]
+
+    def ring_half_copy(s):
+        return remote(
+            part_of(0, 2, s), ring_half.at[s], ring_half_send.at[s], ring_half_recv.at[s], dev_y(-1 if s else 1)
+        )
+
+    def ring_full_copy(k, s, h):
+        return remote(
+            part_of(k, 3 if s else 1, h), ring_full.at[k, s, pl.ds(h * high, high), :],
+            ring_full_send.at[k, s, h], ring_full_recv.at[k, s, h], dev_y(-1 if s else 1),
+        )
+
+    def early_copy(s):
+        return remote(part_of(1, 2, s), early.at[s], early_send.at[s], early_recv.at[s], pair)
+
+    def pair_copy(s):
+        return remote(
+            part_of(1, 0, s), paired.at[pl.ds(s * high, high), :], pair_send.at[s], pair_recv.at[s], pair
+        )
+
+    def give_block(k, dy):
+        def put(i0, value):
             give[k, dy, pl.ds(i0, hid), :] = value.astype(BF16)
 
-        weight_block(k, dy, 1 - c, put_give)
+        weight_block(k, dy, 1 - c, put)
         give_copy(k, dy).start()
 
-        def put_own(i0, value):
-            block[pl.ds(i0, hid), :] = value
-
-        weight_block(k, dy, c, put_own)
+    def own_block(k, dy):
         give_copy(k, dy).wait_recv()
-        if k == 0 and dy == 0:
-            block[...] = block[...] + take[0, 0].astype(F32)
-            return
-        take[k, dy] = (block[...] + take[k, dy].astype(F32)).astype(BF16)
-        if dy == 2:
-            for s in range(2):
-                ring_half_copy(k, s).start()
-        elif dy != 0:
-            s = dy // 2
-            ring_half_copy(k, s).wait_recv()
-            add_into(take.at[k, dy, pl.ds(s * high, high), :], ring_half.at[k, s])
-            ring_full_copy(k, s).start()
+
+        def put(i0, value):
+            value = value + take[k, dy, pl.ds(i0, hid), :].astype(F32)
+            if k == 0 and dy == 0:
+                block[pl.ds(i0, hid), :] = value
+            else:
+                take[k, dy, pl.ds(i0, hid), :] = value.astype(BF16)
+
+        weight_block(k, dy, c, put)
 
     own = pl.ds(0, tok)
     mine = [
@@ -296,8 +298,11 @@
         pl.semaphore_signal(barrier, inc=1, device_id=dev, device_id_type=MESH)
     lanes = lax.broadcasted_iota(jnp.int32, (tok, LANES), 1)
     table = jnp.zeros((tok, LANES), F32)
-    for k in range(ids_in.shape[1]):
-        table = table + jnp.where(lanes == ids_in[:, k : k + 1], scale_in[:, k : k + 1].astype(F32), 0.0)
+    named = []
+    for k in range(ids_in.shape[0]):
+        named.append(jnp.broadcast_to(ids_in[k : k + 1, :], (LANES, tok)).T)
+        scale = jnp.broadcast_to(scale_in[k : k + 1, :].astype(F32), (LANES, tok)).T
+        table = table + jnp.where(lanes == named[k], scale, 0.0)
     rows[own, pl.ds(2 * dim, LANES)] = table.astype(BF16)
     pl.semaphore_wait(barrier, 7)
     for copy in mine:
@@ -324,21 +329,25 @@
     arrived(0, 2, 1, 0)
     arrived(0, 2, 1, 1)
     over(2, 1)
+    arrived(1, 0, 1)
     weights_second()
+    forward(0, 0, 2 * tok)
     for dx in (1, 3):
         arrived(1, dx, 0)
         onward(1, dx, 0)
-    arrived(1, 0, 1)
     arrived(1, 1, 1)
 
     two = 2 * tok
-    forward(0, 0, 2 * two)
+    forward(0, two, two)
     weights_third()
-    arrived(1, 3, 1)
-    forward(0, 2 * two, two)
     weights_last()
     forward(1, 0, 2 * two)
-    forward(1, 2 * two, two)
+    backward(0, 2 * two)
+    for dx in (1, 0):
+        cross_copy(dx).start()
+    arrived(1, 3, 1)
+    for k in range(2):
+        forward(k, 2 * two, two)
     arrived(1, 2, 1)
     for s in range(2):
         arrived(0, 2, 0, s)
@@ -346,50 +355,76 @@
     for k in range(2):
         forward(k, 3 * two, two)
 
-    weight_grad(1, 2)
+    give_block(1, 1)
+    give_block(1, 3)
+    own_block(1, 1)
+    for h in range(2):
+        ring_full_copy(1, 0, h).start()
+    own_block(1, 3)
+    for h in range(2):
+        ring_full_copy(1, 1, h).start()
+    give_block(1, 2)
     backward(3 * two, two)
     cross_copy(2).start()
     send_quarters(1)
     send_quarters(2)
-    weight_grad(1, 1)
+    own_block(1, 2)
+    for s in range(2):
+        early_copy(s).start()
+    give_block(0, 2)
     backward(2 * two, two)
     cross_copy(3).start()
     crossed(2)
     send_quarters(0)
-    weight_grad(1, 3)
-    backward(0, 2 * two)
-    cross_copy(1).start()
-    cross_copy(0).start()
+    own_block(0, 2)
+    give_block(0, 1)
     send_fulls(2)
     send_fulls(1)
-    weight_grad(1, 0)
+    give_block(0, 3)
+    own_block(0, 1)
+    own_block(0, 3)
+    for s in range(2):
+        early_copy(s).wait_recv()
+        add_into(part_of(0, 2, s), early.at[s])
+        ring_half_copy(s).start()
+        ring_full_copy(0, s, 1 - s).start()
+    give_block(1, 0)
     crossed(3)
     crossed(1)
     send_fulls(0)
     settle(2)
     back_copy().start()
-    weight_grad(0, 2)
-    weight_grad(0, 1)
+    own_block(1, 0)
+    for h in range(2):
+        for s in range(2):
+            ring_full_copy(1, s, h).wait_recv()
+        add_into(
+            part_of(1, 0, h), ring_full.at[1, 0, pl.ds(h * high, high), :], ring_full.at[1, 1, pl.ds(h * high, high), :]
+        )
+        pair_copy(h).start()
+    for s in range(2):
+        ring_half_copy(s).wait_recv()
+        add_into(part_of(0, 2 * s + 1, s), ring_half.at[s])
+        ring_full_copy(0, s, s).start()
+    give_block(0, 0)
     settle(1)
-    weight_grad(0, 3)
-    for s in range(2):
-        ring_full_copy(1, s).wait_recv()
-    add_into(take.at[1, 0], ring_full.at[1, 0], ring_full.at[1, 1])
-    pair_copy().start()
     crossed(0)
     settle(0)
-    weight_grad(0, 0)
+    own_block(0, 0)
     back_copy().wait_recv()
     add_into(part.at[place(0, 0, 0), :], back_in)
     input_out[...] = part[own, pl.ds(0, dim)]
     probs = part[own, pl.ds(dim, LANES)].astype(F32)
-    for k in range(ids_in.shape[1]):
-        picked = jnp.where(lanes == ids_in[:, k : k + 1], probs, 0.0)
-        combine_out[:, k : k + 1] = jnp.sum(picked, axis=1, keepdims=True).astype(BF16)
+    for k in range(ids_in.shape[0]):
+        picked = jnp.sum(jnp.where(lanes == named[k], probs, 0.0), axis=1, keepdims=True)
+        combine_out[k : k + 1, :] = jnp.broadcast_to(picked, (tok, LANES)).T[:1]
+    for h in range(2):
+        pair_copy(h).wait_recv()
+    block[...] = block[...] + paired[...].astype(F32)
     for s in range(2):
-        ring_full_copy(0, s).wait_recv()
-    pair_copy().wait_recv()
-    total = block[...] + ring_full[0, 0].astype(F32) + ring_full[0, 1].astype(F32) + paired[...].astype(F32)
+        for h in range(2):
+            ring_full_copy(0, s, h).wait_recv()
+    total = block[...] + ring_full[0, 0].astype(F32) + ring_full[0, 1].astype(F32)
     gu_out[...] = total[: 2 * hid]
     down_out[...] = total[2 * hid :]
 
@@ -410,11 +445,20 @@
         for n in range(3):
             quarter_copy(n, s).wait_send()
             full_copy(n, s).wait_send()
+        ring_half_copy(s).wait_send()
+        early_copy(s).wait_send()
+        pair_copy(s).wait_send()
         for k in range(2):
-            ring_half_copy(k, s).wait_send()
-            ring_full_copy(k, s).wait_send()
+            for h in range(2):
+                ring_full_copy(k, s, h).wait_send()
     back_copy().wait_send()
-    pair_copy().wait_send()
+
+
+def finish(input_in, combine_in, gu_in, down_in, input_out, combine_out, gu_out, down_out):
+    input_out[...] = input_in[...]
+    combine_out[...] = combine_in[...].astype(BF16)
+    gu_out[...] = gu_in[...].T
+    down_out[...] = down_in[...].T
 
 
 def body(activations, out_grad, combine_weights, expert_ids, gate_up_weight, down_weight):
@@ -431,7 +475,7 @@
         kernel,
         out_shape=(
             jax.ShapeDtypeStruct((tok, dim), BF16),
-            jax.ShapeDtypeStruct((tok, top), BF16),
+            jax.ShapeDtypeStruct((top, tok), F32),
             jax.ShapeDtypeStruct((2 * hid, feat), F32),
             jax.ShapeDtypeStruct((hid, feat), F32),
         ),
@@ -449,22 +493,36 @@
             vmem((tok // 2, wide), BF16),
             vmem((2, 4, 3 * hid, feat), BF16),
             vmem((2, 4, 3 * hid, feat), BF16),
-            vmem((2, 2, 3 * hid // 2, feat), BF16),
+            vmem((2, 3 * hid // 2, feat), BF16),
             vmem((2, 2, 3 * hid, feat), BF16),
+            vmem((2, 3 * hid // 2, feat), BF16),
             vmem((3 * hid, feat), BF16),
             vmem((3 * hid, feat), F32),
             dma((4,)),
             dma((2, 4, 2, 2)), dma((2, 4, 2, 2)),
             dma((4, 2, 2)), dma((4, 2, 2)),
             dma((4,)), dma((4,)), dma((3, 2)), dma((3, 2)), dma((3, 2)), dma((3, 2)), dma((1,)), dma((1,)),
-            dma((2, 4)), dma((2, 4)), dma((2, 2)), dma((2, 2)), dma((2, 2)), dma((2, 2)), dma((1,)), dma((1,)),
+            dma((2, 4)), dma((2, 4)), dma((2,)), dma((2,)), dma((2, 2, 2)), dma((2, 2, 2)),
+            dma((2,)), dma((2,)), dma((2,)), dma((2,)),
         ],
         compiler_params=pltpu.CompilerParams(
             collective_id=0, has_side_effects=True, vmem_limit_bytes=67043328
         ),
         name="routed",
-    )(activations, out_grad, expert_ids, combine_weights, gate_up_weight[0], down_weight[0])
-    return (grad_input, grad_combine, grad_gu.T[None], grad_down.T[None])
+    )(activations, out_grad, expert_ids.T, combine_weights.T, gate_up_weight[0], down_weight[0])
+    grad_input, grad_combine, grad_gu, grad_down = pl.pallas_call(
+        finish,
+        out_shape=(
+            jax.ShapeDtypeStruct((tok, dim), BF16),
+            jax.ShapeDtypeStruct((top, tok), BF16),
+            jax.ShapeDtypeStruct((feat, 2 * hid), F32),
+            jax.ShapeDtypeStruct((feat, hid), F32),
+        ),
+        in_specs=[whole] * 4,
+        out_specs=[whole] * 4,
+        name="finish",
+    )(grad_input, grad_combine, grad_gu, grad_down)
+    return (grad_input, grad_combine.T, grad_gu[None], grad_down[None])
 
 
 def solution(mesh):

time: 160 us -> 140 us (0.88)
  local copies, waits for them, and re-layouts: 10.7 us -> 0 us
  Pallas kernels: 148 us -> 139 us
    pallas_call x1, Pallas kernels: 148 us -> 136 us  [body(): pl.pallas_call(kernel, out_shape=(jax.ShapeDtypeStruct((tok, dim), BF16),...]
    unnamed x6 -> x0, local copies, waits for them, and re-layouts: 10.7 us -> none
    pallas_call x0 -> x1, Pallas kernels: none -> 3.21 us  [body(): pl.pallas_call(finish, out_shape=(jax.ShapeDtypeStruct((tok, dim), BF16),...]
where the time goes in v4:
time: 140 us; the launch traced here: 139 us
  Pallas kernels  139 us (99%)
    pallas_call x1, Pallas kernels, body(): pl.pallas_call(kernel, out_shape=(jax.ShapeDtypeStruct((tok, dim), BF16),...  136 us
    pallas_call x1, Pallas kernels, body(): pl.pallas_call(finish, out_shape=(jax.ShapeDtypeStruct((tok, dim), BF16),...  3.21 us

profile of v4, /device:TPU:1, one launch (start us, length us, event | category | flops | bytes accessed | tf_op | source)
XLA Modules:
  0.0 139.4 jit_solution(9823160360968157073)
XLA Ops:
  0.6 135.5 %routed.1 = (bf16[128,2048]{1,0:T(8,128)(2,1)}, f32[4,128]{1,0:T(4,128)}, f32[1024,256]{1,0:T(8,128)}, f32[512,256]{1,0:T(8,128)}) custom-call(bf16[128,2048]{1,0:T(8,128)(2,1)} %x_in.1, bf16[128,2048]{1,0:T(8,128)(2,1)} %g_in.1, s32[4,128]{1,0:T(4,128)} %bitcast.9, bf16[4,128]{1,0:T(4,128)(2,1)} %bitcast.10, bf16[2048,1024]{1,0:T(8,128)(2,1)} %bitcast.7, ...), custom_call_target="tpu_custom_call" | custom-call | tf_op jit(solution)/shard_map/routed/pallas_call | solution.py:474
  136.2 3.2 %finish.1 = (bf16[128,2048]{1,0:T(8,128)(2,1)}, bf16[4,128]{1,0:T(4,128)(2,1)}, f32[256,1024]{1,0:T(8,128)}, f32[256,512]{1,0:T(8,128)}) custom-call(bf16[128,2048]{1,0:T(8,128)(2,1)} %get-tuple-element.12.input_in, f32[4,128]{1,0:T(4,128)} %get-tuple-element.13.combine_in, f32[1024,256]{1,0:T(8,128)} %get-tuple-element.14.gu_in, ...), custom_call_target="tpu_custom_call" | custom-call | tf_op jit(solution)/shard_map/finish/pallas_call | solution.py:513
